TPU v7x, 32 devices: a whole 2x2x4 slice. The times are simulated.
32 devices in a mesh: replica: 8 (over z, y), shard: 4 (over x, core).
Axes of the slice: x: 2, y: 2, z: 4, core: 2. Of those that a mesh axis runs over, the one named last changes fastest.
Arguments:
- tokens: bfloat16 [16, 512, 768], P('replica', 'shard'), may hold values from -6 to 6
- cotangent: bfloat16 [16, 512, 768], P('replica', 'shard'), may hold values from -6 to 6
- clip_count: int32 [8], P('replica'), may hold values from 1 to 2, as said below
- ln1_gain: float32 [768], P('shard'), may hold values from 0.5 to 1.5
- ln1_bias: float32 [768], P('shard'), may hold values from -3 to 3
- qkv_weight: float32 [768, 2304], P('shard'), may hold values from -0.21875 to 0.21875
- q_bias: float32 [768], P('shard'), may hold values from -3 to 3
- v_bias: float32 [768], P('shard'), may hold values from -3 to 3
- out_weight: float32 [768, 768], P('shard'), may hold values from -0.875 to 0.875
- out_bias: float32 [768], P('shard'), may hold values from -3 to 3
- ln2_gain: float32 [768], P('shard'), may hold values from 0.5 to 1.5
- ln2_bias: float32 [768], P('shard'), may hold values from -3 to 3
- fc1_weight: float32 [768, 3072], P('shard'), may hold values from -0.21875 to 0.21875
- fc1_bias: float32 [3072], P('shard'), may hold values from -3 to 3
- fc2_weight: float32 [3072, 768], P('shard'), may hold values from -0.109375 to 0.109375
- fc2_bias: float32 [768], P('shard'), may hold values from -3 to 3
Outputs:
- outputs: bfloat16 [16, 512, 768], P('replica', 'shard')
- input_grad: float32 [16, 512, 768], P('replica', 'shard')
- ln1_gain_grad: float32 [768], P('shard')
- ln1_bias_grad: float32 [768], P('shard')
- qkv_weight_grad: float32 [768, 2304], P('shard')
- q_bias_grad: float32 [768], P('shard')
- v_bias_grad: float32 [768], P('shard')
- out_weight_grad: float32 [768, 768], P('shard')
- out_bias_grad: float32 [768], P('shard')
- ln2_gain_grad: float32 [768], P('shard')
- ln2_bias_grad: float32 [768], P('shard')
- fc1_weight_grad: float32 [768, 3072], P('shard')
- fc1_bias_grad: float32 [3072], P('shard')
- fc2_weight_grad: float32 [3072, 768], P('shard')
- fc2_bias_grad: float32 [768], P('shard')
Inputs may be any that keep to these rules, and one draw needn't show every extreme that they name: Clip slots 0 to clip_count[r] - 1 of replica group r are live, the rest are padding; some group has 2 live slots and some group one.
All inputs are finite; a program needn't handle non-finite values.
Results may differ from a plain program's by a relative error of at most 0.015.
Values may be sent and summed in bfloat16 or wider, within the bound.
A program may use at most 192 MiB of HBM per device.

v0:
```python
import jax
import jax.numpy as jnp
from jax import lax
from jax.sharding import PartitionSpec as P

D = 768
HEADS = 12
HD = 64


EPSILON = 1e-06


def layer_norm(values, gain, shift):
    mean_value = jnp.mean(values, axis=-1, keepdims=True)
    centred = values - mean_value
    spread = jnp.mean(centred * centred, axis=-1, keepdims=True)
    return centred * lax.rsqrt(spread + EPSILON) * gain + shift


def exact_gelu(values):
    return jax.nn.gelu(values, approximate=False)


def multiply(left, right):
    return jnp.dot(left, right, preferred_element_type=jnp.float32)


def multiply_over_rows(left, right):
    return lax.dot_general(
        left, right, (((0,), (0,)), ((), ())), preferred_element_type=jnp.float32
    )


def multiply_by_transpose(left, right):
    return lax.dot_general(
        left, right, (((1,), (1,)), ((), ())), preferred_element_type=jnp.float32
    )


def scaled_scores(query_heads, key_heads):
    return jnp.einsum(
        "qhd,khd->hqk", query_heads, key_heads, preferred_element_type=jnp.float32
    ) * HD ** (-0.5)


def column_sums(values):
    return jnp.sum(values.astype(jnp.float32), axis=0)


def local(
    tokens,
    cotangent,
    clip_count,
    ln1_gain,
    ln1_bias,
    qkv_weight,
    q_bias,
    v_bias,
    out_weight,
    out_bias,
    ln2_gain,
    ln2_bias,
    fc1_weight,
    fc1_bias,
    fc2_weight,
    fc2_bias,
):
    brain = jnp.bfloat16
    single = jnp.float32
    slot_count = tokens.shape[0]
    local_tokens = tokens.shape[1]
    seq_length = local_tokens * lax.axis_size("shard")
    all_rows = slot_count * local_tokens
    live_slots = (jnp.arange(slot_count) < clip_count[0]).astype(single)
    live_rows = jnp.repeat(live_slots, local_tokens)[:, None]
    gain_one, shift_one, weight_qkv, bias_query, bias_value, weight_out, bias_out = (
        lax.all_gather(ln1_gain.astype(brain), "shard", axis=0, tiled=True),
        lax.all_gather(ln1_bias.astype(brain), "shard", axis=0, tiled=True),
        lax.all_gather(qkv_weight.astype(brain), "shard", axis=0, tiled=True),
        lax.all_gather(q_bias.astype(brain), "shard", axis=0, tiled=True),
        lax.all_gather(v_bias.astype(brain), "shard", axis=0, tiled=True),
        lax.all_gather(out_weight.astype(brain), "shard", axis=0, tiled=True),
        lax.all_gather(out_bias.astype(brain), "shard", axis=0, tiled=True),
    )
    inputs = tokens.reshape(all_rows, D).astype(single)
    hidden_one = layer_norm(inputs, gain_one.astype(single), shift_one.astype(single)).astype(brain)
    projected = multiply(hidden_one, weight_qkv)
    queries = (projected[:, :D] + bias_query.astype(single)).astype(brain)
    keys_local = projected[:, D : 2 * D].astype(brain)
    values_local = (projected[:, 2 * D :] + bias_value.astype(single)).astype(brain)
    pairs_local = jnp.concatenate([keys_local, values_local], axis=1).reshape(
        slot_count, local_tokens, 2 * D
    )
    pairs_full = lax.all_gather(pairs_local, "shard", axis=1, tiled=True)
    mixture_parts = []
    log_totals = []
    for slot_index in range(slot_count):
        query_heads = queries[slot_index * local_tokens : (slot_index + 1) * local_tokens].reshape(
            local_tokens, HEADS, HD
        )
        key_heads = pairs_full[slot_index, :, :D].reshape(seq_length, HEADS, HD)
        value_heads = pairs_full[slot_index, :, D:].reshape(seq_length, HEADS, HD)
        scores = scaled_scores(query_heads, key_heads)
        highest = jnp.max(scores, axis=-1, keepdims=True)
        expanded = jnp.exp(scores - highest)
        totals = jnp.sum(expanded, axis=-1, keepdims=True)
        softened = (expanded / totals).astype(brain)
        mixture = jnp.einsum("hqk,khd->qhd", softened, value_heads, preferred_element_type=single)
        mixture_parts.append(mixture.reshape(local_tokens, D))
        log_totals.append(highest + jnp.log(totals))
    attended = jnp.concatenate(mixture_parts, axis=0).astype(brain)
    middle = inputs + multiply(attended, weight_out) + bias_out.astype(single)
    gain_two, shift_two, weight_up, bias_up, weight_down, bias_down = (
        lax.all_gather(ln2_gain.astype(brain), "shard", axis=0, tiled=True),
        lax.all_gather(ln2_bias.astype(brain), "shard", axis=0, tiled=True),
        lax.all_gather(fc1_weight.astype(brain), "shard", axis=0, tiled=True),
        lax.all_gather(fc1_bias.astype(brain), "shard", axis=0, tiled=True),
        lax.all_gather(fc2_weight.astype(brain), "shard", axis=0, tiled=True),
        lax.all_gather(fc2_bias.astype(brain), "shard", axis=0, tiled=True),
    )
    hidden_two = layer_norm(middle, gain_two.astype(single), shift_two.astype(single)).astype(brain)
    lifted = multiply(hidden_two, weight_up) + bias_up.astype(single)
    activated = exact_gelu(lifted).astype(brain)
    result = middle + multiply(activated, weight_down) + bias_down.astype(single)
    outputs = (result * live_rows).astype(brain).reshape(slot_count, local_tokens, D)
    grad_output = cotangent.reshape(all_rows, D).astype(single) * live_rows
    grad_branch_two = grad_output.astype(brain)
    grad_down = multiply_over_rows(activated, grad_branch_two)
    grad_bias_down = column_sums(grad_branch_two)
    grad_activated = multiply_by_transpose(grad_branch_two, weight_down)
    unused_gelu, gelu_back = jax.vjp(exact_gelu, lifted)
    grad_lifted = gelu_back(grad_activated)[0].astype(brain)
    grad_up = multiply_over_rows(hidden_two, grad_lifted)
    grad_bias_up = column_sums(grad_lifted)
    grad_hidden_two = multiply_by_transpose(grad_lifted, weight_up)
    unused_two, norm_back_two = jax.vjp(
        layer_norm, middle, gain_two.astype(single), shift_two.astype(single)
    )
    grad_middle_part, grad_gain_two, grad_shift_two = norm_back_two(grad_hidden_two)
    grad_middle = grad_output + grad_middle_part
    sum_gain_two, sum_shift_two, sum_up, sum_bias_up, sum_down, sum_bias_down = (
        lax.psum_scatter(
            grad_gain_two.astype(jnp.bfloat16), "shard", scatter_dimension=0, tiled=True
        ).astype(jnp.float32),
        lax.psum_scatter(
            grad_shift_two.astype(jnp.bfloat16), "shard", scatter_dimension=0, tiled=True
        ).astype(jnp.float32),
        lax.psum_scatter(
            grad_up.astype(jnp.bfloat16), "shard", scatter_dimension=0, tiled=True
        ).astype(jnp.float32),
        lax.psum_scatter(
            grad_bias_up.astype(jnp.bfloat16), "shard", scatter_dimension=0, tiled=True
        ).astype(jnp.float32),
        lax.psum_scatter(
            grad_down.astype(jnp.bfloat16), "shard", scatter_dimension=0, tiled=True
        ).astype(jnp.float32),
        lax.psum_scatter(
            grad_bias_down.astype(jnp.bfloat16), "shard", scatter_dimension=0, tiled=True
        ).astype(jnp.float32),
    )
    grad_branch_one = grad_middle.astype(brain)
    grad_weight_out = multiply_over_rows(attended, grad_branch_one)
    grad_bias_out = column_sums(grad_branch_one)
    grad_attended = multiply_by_transpose(grad_branch_one, weight_out).astype(brain)
    grad_query_parts = []
    grad_pair_parts = []
    inner_parts = []
    for slot_index in range(slot_count):
        query_heads = queries[slot_index * local_tokens : (slot_index + 1) * local_tokens].reshape(
            local_tokens, HEADS, HD
        )
        key_heads = pairs_full[slot_index, :, :D].reshape(seq_length, HEADS, HD)
        value_heads = pairs_full[slot_index, :, D:].reshape(seq_length, HEADS, HD)
        grad_heads = grad_attended[
            slot_index * local_tokens : (slot_index + 1) * local_tokens
        ].reshape(local_tokens, HEADS, HD)
        scores = scaled_scores(query_heads, key_heads)
        softened = jnp.exp(scores - log_totals[slot_index])
        grad_softened = jnp.einsum(
            "qhd,khd->hqk", grad_heads, value_heads, preferred_element_type=single
        )
        inner_sum = jnp.sum(grad_softened * softened, axis=-1, keepdims=True)
        inner_parts.append(inner_sum[:, :, 0])
        grad_scores = (softened * (grad_softened - inner_sum)).astype(brain)
        grad_query = jnp.einsum(
            "hqk,khd->qhd", grad_scores, key_heads, preferred_element_type=single
        ) * HD ** (-0.5)
        grad_query_parts.append(grad_query.reshape(local_tokens, D))
        grad_key = jnp.einsum(
            "hqk,qhd->khd", grad_scores, query_heads, preferred_element_type=single
        ) * HD ** (-0.5)
        grad_value = jnp.einsum(
            "hqk,qhd->khd", softened.astype(brain), grad_heads, preferred_element_type=single
        )
        grad_pair_parts.append(
            jnp.concatenate(
                [grad_key.reshape(seq_length, D), grad_value.reshape(seq_length, D)], axis=1
            )
        )
    grad_pairs_full = jnp.stack(grad_pair_parts, axis=0)
    grad_pairs = (
        lax.psum_scatter(
            grad_pairs_full.astype(jnp.bfloat16), "shard", scatter_dimension=1, tiled=True
        )
        .astype(jnp.float32)
        .astype(brain)
        .reshape(all_rows, 2 * D)
    )
    grad_queries = jnp.concatenate(grad_query_parts, axis=0).astype(brain)
    grad_projected = jnp.concatenate([grad_queries, grad_pairs], axis=1)
    grad_qkv = multiply_over_rows(hidden_one, grad_projected)
    grad_bias_query = column_sums(grad_queries)
    grad_bias_value = column_sums(grad_pairs[:, D:])
    grad_hidden_one = multiply_by_transpose(grad_projected, weight_qkv)
    unused_one, norm_back_one = jax.vjp(
        layer_norm, inputs, gain_one.astype(single), shift_one.astype(single)
    )
    grad_inputs_part, grad_gain_one, grad_shift_one = norm_back_one(grad_hidden_one)
    input_grad = (grad_middle + grad_inputs_part).reshape(slot_count, local_tokens, D)
    (
        sum_gain_one,
        sum_shift_one,
        sum_qkv,
        sum_bias_query,
        sum_bias_value,
        sum_weight_out,
        sum_bias_out,
    ) = (
        lax.psum_scatter(
            grad_gain_one.astype(jnp.bfloat16), "shard", scatter_dimension=0, tiled=True
        ).astype(jnp.float32),
        lax.psum_scatter(
            grad_shift_one.astype(jnp.bfloat16), "shard", scatter_dimension=0, tiled=True
        ).astype(jnp.float32),
        lax.psum_scatter(
            grad_qkv.astype(jnp.bfloat16), "shard", scatter_dimension=0, tiled=True
        ).astype(jnp.float32),
        lax.psum_scatter(
            grad_bias_query.astype(jnp.bfloat16), "shard", scatter_dimension=0, tiled=True
        ).astype(jnp.float32),
        lax.psum_scatter(
            grad_bias_value.astype(jnp.bfloat16), "shard", scatter_dimension=0, tiled=True
        ).astype(jnp.float32),
        lax.psum_scatter(
            grad_weight_out.astype(jnp.bfloat16), "shard", scatter_dimension=0, tiled=True
        ).astype(jnp.float32),
        lax.psum_scatter(
            grad_bias_out.astype(jnp.bfloat16), "shard", scatter_dimension=0, tiled=True
        ).astype(jnp.float32),
    )
    (
        sum_gain_one,
        sum_shift_one,
        sum_qkv,
        sum_bias_query,
        sum_bias_value,
        sum_weight_out,
        sum_bias_out,
        sum_gain_two,
        sum_shift_two,
        sum_up,
        sum_bias_up,
        sum_down,
        sum_bias_down,
    ) = lax.psum(
        (
            sum_gain_one,
            sum_shift_one,
            sum_qkv,
            sum_bias_query,
            sum_bias_value,
            sum_weight_out,
            sum_bias_out,
            sum_gain_two,
            sum_shift_two,
            sum_up,
            sum_bias_up,
            sum_down,
            sum_bias_down,
        ),
        "replica",
    )
    return (
        outputs,
        input_grad,
        sum_gain_one,
        sum_shift_one,
        sum_qkv,
        sum_bias_query,
        sum_bias_value,
        sum_weight_out,
        sum_bias_out,
        sum_gain_two,
        sum_shift_two,
        sum_up,
        sum_bias_up,
        sum_down,
        sum_bias_down,
    )


def solution(mesh):
    return jax.shard_map(
        local,
        mesh=mesh,
        in_specs=(
            P("replica", "shard", None),
            P("replica", "shard", None),
            P("replica"),
            P("shard"),
            P("shard"),
            P("shard", None),
            P("shard"),
            P("shard"),
            P("shard", None),
            P("shard"),
            P("shard"),
            P("shard"),
            P("shard", None),
            P("shard"),
            P("shard", None),
            P("shard"),
        ),
        out_specs=(
            P("replica", "shard", None),
            P("replica", "shard", None),
            P("shard"),
            P("shard"),
            P("shard", None),
            P("shard"),
            P("shard"),
            P("shard", None),
            P("shard"),
            P("shard"),
            P("shard"),
            P("shard", None),
            P("shard"),
            P("shard", None),
            P("shard"),
        ),
        check_vma=False,
    )
```

profile of v0, /device:TPU:0, one launch (start us, length us, event | category | flops | bytes accessed | tf_op | source)
XLA Modules:
  0.0 728.4 jit_solution(6335136803925444801)
XLA Ops:
  7.3 2.5 convert_element_type.228
  12.8 13.1 %all-reduce.19 = (bf16[768]{0:T(1024)(128)(2,1)S(1)}, bf16[768]{0:T(1024)(128)(2,1)S(1)}, bf16[768]{0:T(1024)(128)(2,1)S(1)}, bf16[768]{0:T(1024)(128)(2,1)S(1)}...) all-reduce(bf16[768]{0:T(1024)(128)(2,1)S(1)} %dynamic-update-slice, ...), channel_id=1, replica_groups=mesh['replica'=8,'shard'=4] {'shard'}, use_global_device_ids=true, to_apply=%add.4 | all-reduce | flops 5376 | bytes 21504
  27.2 16.5 %all-gather.7.cloned.1.call-done = bf16[768,2304]{1,0:T(8,128)(2,1)} async-done(((bf16[192,2304]{1,0:T(8,128)(2,1)}), bf16[768,2304]{1,0:T(8,128)(2,1)}) %all-gather.7.cloned.1.call-update) | async-done | bytes 3538960 | tf_op jit(solution)/shard_map/all_gather | solution.py:80
  43.8 3.1 fusion.62
  48.1 1.8 convert_element_type.237
  50.0 1.2 convert_element_type.245
  51.3 2.8 convert_element_type.249
  55.5 5.2 all-gather
  63.9 13.0 %all-gather.9.cloned.1.call-done = bf16[2,512,1536]{2,1,0:T(8,128)(2,1)} async-done(((bf16[2,128,1536]{2,1,0:T(8,128)(2,1)}), bf16[2,512,1536]{2,1,0:T(8,128)(2,1)}) %all-gather.9.cloned.1.call-update) | async-done | bytes 3145744 | tf_op jit(solution)/shard_map/all_gather | solution.py:95
  76.8 2.0 fusion.57
  80.1 1.2 copy.63
  81.2 1.2 copy.61
  83.5 2.0 multiply_reduce_fusion.2
  88.2 2.0 fusion.32
  90.3 1.9 fusion.33
  92.2 3.7 all-gather.11.cloned.1.call-done
  95.9 2.1 fusion.61
  100.9 34.5 %all-gather.13.cloned.1.call-done = bf16[768,3072]{1,0:T(8,128)(2,1)} async-done(((bf16[192,3072]{1,0:T(8,128)(2,1)}), bf16[768,3072]{1,0:T(8,128)(2,1)}) %all-gather.13.cloned.1.call-update) | async-done | bytes 4718608 | tf_op jit(solution)/shard_map/all_gather | solution.py:117
  135.4 5.7 convolution_add_fusion
  141.1 33.8 %all-gather.15.cloned.1.call-done = bf16[3072,768]{1,0:T(8,128)(2,1)} async-done(((bf16[768,768]{1,0:T(8,128)(2,1)}), bf16[3072,768]{1,0:T(8,128)(2,1)}) %all-gather.15.cloned.1.call-update) | async-done | bytes 4718608 | tf_op jit(solution)/shard_map/all_gather | solution.py:119
  174.9 12.5 %fusion.52 = (bf16[3072]{0:T(1024)(128)(2,1)}, bf16[256,3072]{1,0:T(8,128)(2,1)S(1)}, f32[256,3072]{1,0:T(8,128)}) fusion(f32[256,3072]{1,0:T(8,128)} %convolution_add_fusion, bf16[256,768]{1,0:T(8,128)(2,1)} %fusion.36, bf16[3072,768]{1,0:T(8,128)(2,1)} %all-gather.15.cloned.1.call-done), kind=kOutput, calls=%fused_computation.132 | convolution fusion | flops 1265366016 | bytes 12982272 | tf_op jit(solution)/shard_map/dot_general | solution.py:36
  187.4 2.3 multiply_reduce_fusion.4
  193.7 1.8 copy.64
  195.5 3.7 fusion.20
  199.3 3.3 multiply_reduce_fusion.1
  202.5 1.8 copy.65
  204.3 2.7 fusion.23
  207.0 3.2 multiply_reduce_fusion
  210.3 2.3 copy.71
  212.6 2.3 copy.69
  214.9 3.3 multiply_convert_fusion.1
  219.3 1.2 multiply_convert_fusion.4
  220.6 2.3 copy.68
  222.9 2.4 multiply_convert_fusion
  226.4 1.3 multiply_convert_fusion.3
  227.7 1.4 copy.70
  229.4 2.0 pad_maximum_fusion
  232.5 1.5 convolution_convert_fusion.3
  234.2 3.7 convolution_convert_fusion.1
  238.2 2.0 copy-done.29
  240.2 2.6 multiply_convert_fusion.2
  244.0 3.6 convolution_convert_fusion
  247.6 1.3 copy-done.3
  249.0 2.7 bitcast_reduce_fusion.1
  252.8 1.9 bitcast_reduce_fusion
  254.8 14.8 %reduce-scatter.6.cloned.1.call-done = bf16[2,128,1536]{2,1,0:T(8,128)(2,1)} async-done(((bf16[2,512,1536]{2,1,0:T(8,128)(2,1)}), bf16[2,128,1536]{2,1,0:T(8,128)(2,1)}) %reduce-scatter.6.cloned.1.call-update) | async-done | bytes 786448 | tf_op jit(solution)/shard_map/reduce_scatter | solution.py:203
  269.6 4.1 convolution_convert_fusion.2
  276.8 21.2 %reduce-scatter.10.cloned.1.call-done = bf16[192,768]{1,0:T(8,128)(2,1)} async-done(((bf16[768,768]{1,0:T(8,128)(2,1)}), bf16[192,768]{1,0:T(8,128)(2,1)}) %reduce-scatter.10.cloned.1.call-update) | async-done | bytes 294928 | tf_op jit(solution)/shard_map/reduce_scatter | solution.py:245
  298.8 3.9 fusion.51
  304.5 11.5 %all-reduce.18 = (bf16[768]{0:T(1024)(128)(2,1)}, bf16[768]{0:T(1024)(128)(2,1)}, bf16[768]{0:T(1024)(128)(2,1)}, bf16[768]{0:T(1024)(128)(2,1)}, bf16[768]{0:T(...) all-reduce(bf16[768]{0:T(1024)(128)(2,1)} %copy-done.75, ...), channel_id=1, replica_groups=mesh['replica'=8,'shard'=4] {'shard'}, use_global_device_ids=true, to_apply=%add.7 | all-reduce | flops 9984 | bytes 39936
  316.7 1.3 dynamic-slice_convert_fusion.8
  318.0 1.3 dynamic-slice_convert_fusion.7
  319.3 1.3 dynamic-slice_convert_fusion.6
  320.7 1.3 dynamic-slice_convert_fusion.5
  322.0 1.3 dynamic-slice_convert_fusion.4
  323.3 1.3 dynamic-slice_convert_fusion.3
  324.6 1.3 dynamic-slice_convert_fusion.2
  325.9 1.3 dynamic-slice_convert_fusion.1
  328.6 2.6 add_add_fusion.2
  331.3 4.6 fusion.29
  335.9 12.6 %reduce-scatter.12.cloned.1.call-done = bf16[192,3072]{1,0:T(8,128)(2,1)} async-done(((bf16[768,3072]{1,0:T(8,128)(2,1)}), bf16[192,3072]{1,0:T(8,128)(2,1)}) %reduce-scatter.12.cloned.1.call-update) | async-done | bytes 1179664 | tf_op jit(solution)/shard_map/reduce_scatter | solution.py:149
  348.5 50.6 %reduce-scatter.14.cloned.1.call-done = bf16[768,768]{1,0:T(8,128)(2,1)} async-done(((bf16[3072,768]{1,0:T(8,128)(2,1)}), bf16[768,768]{1,0:T(8,128)(2,1)}) %reduce-scatter.14.cloned.1.call-update) | async-done | bytes 1179664 | tf_op jit(solution)/shard_map/reduce_scatter | solution.py:155
  399.1 42.9 %reduce-scatter.8.cloned.1.call-done = bf16[192,2304]{1,0:T(8,128)(2,1)} async-done(((bf16[768,2304]{1,0:T(8,128)(2,1)}), bf16[192,2304]{1,0:T(8,128)(2,1)}) %reduce-scatter.8.cloned.1.call-update) | async-done | bytes 884752 | tf_op jit(solution)/shard_map/reduce_scatter | solution.py:236
  442.1 279.0 %all-reduce.21 = (f32[192]{0:T(256)}, f32[192]{0:T(256)}, f32[192,2304]{1,0:T(8,128)}, f32[192]{0:T(256)}, f32[192]{0:T(256)}, /*index=5*/f32[192,768]{1,0:T(8,1...) all-reduce(f32[192]{0:T(256)S(1)} %copy-done.78, ...), channel_id=1, replica_groups=mesh['replica'=8,'shard'=4] {'replica'}, use_global_device_ids=true, to_apply=%region_17.0 | all-reduce | flops 1771776 | bytes 10635264 | tf_op jit(solution)/shard_map/psum | solution.py:266
  (291 shorter events, 33.3 us)
Async XLA Ops:
  7.2 2.9 copy-start.86
  7.2 2.8 copy-start.95
  7.3 2.8 copy-start.96
  7.3 18.7 %copy-start.6 = (bf16[2,128,768]{2,1,0:T(8,128)(2,1)S(1)}, bf16[2,128,768]{2,1,0:T(8,128)(2,1)}, u32[]{:S(2)}) copy-start(bf16[2,128,768]{2,1,0:T(8,128)(2,1)} %param.16) | copy-start | bytes 1179652
  7.3 36.5 %all-gather.7.cloned.1.call-start = ((), (), s32[]{:S(2)}) async-start(), calls=%async_computation.5 | async-start | bytes 4423680 | tf_op jit(solution)/shard_map/all_gather | solution.py:80
  9.9 67.0 %all-gather.9.cloned.1.call-start = ((), (), s32[]{:S(2)}) async-start(), calls=%async_computation.6 | async-start | bytes 3932160 | tf_op jit(solution)/shard_map/all_gather | solution.py:95
  26.4 20.5 %copy-start.70 = (f32[2,128]{1,0:T(2,128)}, f32[2,128]{1,0:T(2,128)S(1)}, u32[]{:S(2)}) copy-start(f32[2,128]{1,0:T(2,128)S(1)} %multiply_reduce_fusion.9) | copy-start | bytes 3076
  27.2 19.7 %copy-start.37 = (bf16[256,768]{1,0:T(8,128)(2,1)}, bf16[256,768]{1,0:T(8,128)(2,1)S(1)}, u32[]{:S(2)}) copy-start(bf16[256,768]{1,0:T(8,128)(2,1)S(1)} %add_convert_fusion.2) | copy-start | bytes 1179652
  46.9 3.1 copy-start.30
  48.0 47.9 %all-gather.11.cloned.1.call-start = ((), (), s32[]{:S(2)}) async-start(), calls=%async_computation.7 | async-start | bytes 1474560 | tf_op jit(solution)/shard_map/all_gather | solution.py:83
  50.0 85.4 %all-gather.13.cloned.1.call-start = ((), (), s32[]{:S(2)}) async-start(), calls=%async_computation.8 | async-start | bytes 5898240 | tf_op jit(solution)/shard_map/all_gather | solution.py:117
  51.2 3.7 copy-start.76
  51.2 10.1 %copy-start.16 = (bf16[2,128,768]{2,1,0:T(8,128)(2,1)S(1)}, bf16[2,128,768]{2,1,0:T(8,128)(2,1)}, u32[]{:S(2)}) copy-start(bf16[2,128,768]{2,1,0:T(8,128)(2,1)} %param.17) | copy-start | bytes 1179652
  51.2 123.7 %all-gather.15.cloned.1.call-start = ((), (), s32[]{:S(2)}) async-start(), calls=%async_computation.9 | async-start | bytes 5898240 | tf_op jit(solution)/shard_map/all_gather | solution.py:119
  54.1 215.4 %reduce-scatter.6.cloned.1.call-start = ((), (), s32[]{:S(2)}) async-start(), calls=%async_computation.10 | async-start | bytes 3932160 | tf_op jit(solution)/shard_map/reduce_scatter | solution.py:203
  61.2 17.7 %copy-start.87 = (f32[2]{0:T(128)}, f32[2]{0:T(128)S(1)}, u32[]{:S(2)}) copy-start(f32[2]{0:T(128)S(1)} %compare_convert_fusion) | copy-start | bytes 28
  61.3 17.6 %copy-start.66 = (f32[256]{0:T(256)}, f32[256]{0:T(256)S(1)}, u32[]{:S(2)}) copy-start(f32[256]{0:T(256)S(1)} %broadcast_bitcast_fusion) | copy-start | bytes 3076
  83.5 2.9 copy-start.15
  83.5 3.0 copy-start.32
  87.2 3.0 copy-start
  87.2 3.0 copy-start.49
  90.3 5.7 copy-start.77
  95.9 4.4 copy-start.48
  95.9 4.4 copy-start.54
  95.9 4.4 copy-start.50
  95.9 4.4 copy-start.56
  174.9 12.5 %copy-start.10 = (f32[256,768]{1,0:T(8,128)S(1)}, f32[256,768]{1,0:T(8,128)}, u32[]{:S(2)}) copy-start(f32[256,768]{1,0:T(8,128)} %copy-done.9) | copy-start | bytes 2359300
  174.9 12.5 %copy-start.58 = (f32[256]{0:T(256)S(1)}, f32[256]{0:T(256)}, u32[]{:S(2)}) copy-start(f32[256]{0:T(256)} %copy-done.57) | copy-start | bytes 3076
  174.9 12.5 %copy-start.64 = (f32[256]{0:T(256)S(1)}, f32[256]{0:T(256)}, u32[]{:S(2)}) copy-start(f32[256]{0:T(256)} %fusion.40) | copy-start | bytes 3076
  174.9 12.5 %copy-start.89 = (bf16[768,3072]{1,0:T(8,128)(2,1)S(1)}, bf16[768,3072]{1,0:T(8,128)(2,1)}, u32[]{:S(2)}) copy-start(bf16[768,3072]{1,0:T(8,128)(2,1)} %all-gather.13.cloned.1.call-done) | copy-start | bytes 14155780
  187.4 3.5 copy-start.17
  187.4 3.5 copy-start.67
  195.5 3.7 copy-start.1
  195.5 3.7 copy-start.24
  195.5 3.7 copy-start.34
  195.5 3.8 copy-start.46
  214.9 4.5 copy-start.33
  222.9 3.5 copy-start.31
  231.5 66.6 %reduce-scatter.10.cloned.1.call-start = ((), (), s32[]{:S(2)}) async-start(), calls=%async_computation.12 | async-start | bytes 1474560 | tf_op jit(solution)/shard_map/reduce_scatter | solution.py:245
  234.1 114.4 %reduce-scatter.12.cloned.1.call-start = ((), (), s32[]{:S(2)}) async-start(), calls=%async_computation.13 | async-start | bytes 5898240 | tf_op jit(solution)/shard_map/reduce_scatter | solution.py:149
  237.9 161.2 %reduce-scatter.14.cloned.1.call-start = ((), (), s32[]{:S(2)}) async-start(), calls=%async_computation.14 | async-start | bytes 5898240 | tf_op jit(solution)/shard_map/reduce_scatter | solution.py:155
  240.2 3.8 copy-start.36
  247.6 5.2 copy-start.5
  247.6 194.4 %reduce-scatter.8.cloned.1.call-start = ((), (), s32[]{:S(2)}) async-start(), calls=%async_computation.11 | async-start | bytes 4423680 | tf_op jit(solution)/shard_map/reduce_scatter | solution.py:236
  251.6 18.0 %copy-start.38 = (bf16[256,768]{1,0:T(8,128)(2,1)S(1)}, bf16[256,768]{1,0:T(8,128)(2,1)}, u32[]{:S(2)}) copy-start(bf16[256,768]{1,0:T(8,128)(2,1)} %copy-done.37) | copy-start | bytes 1179652
  273.6 24.4 %copy-start.43 = (bf16[2,128,1536]{2,1,0:T(8,128)(2,1)S(1)}, bf16[2,128,1536]{2,1,0:T(8,128)(2,1)}, u32[]{:S(2)}) copy-start(bf16[2,128,1536]{2,1,0:T(8,128)(2,1)} %reduce-scatter.6.cloned.1.call-done) | copy-start | bytes 2359300
  273.7 25.1 %copy-start.52 = (f32[768]{0:T(1024)S(1)}, f32[768]{0:T(1024)}, u32[]{:S(2)}) copy-start(f32[768]{0:T(1024)} %copy-done.51) | copy-start | bytes 9220
  273.7 25.1 %copy-start.61 = (f32[256]{0:T(256)S(1)}, f32[256]{0:T(256)}, u32[]{:S(2)}) copy-start(f32[256]{0:T(256)} %copy-done.60) | copy-start | bytes 3076
  275.4 22.7 %copy-start.75 = (bf16[768]{0:T(1024)(128)(2,1)}, bf16[768]{0:T(1024)(128)(2,1)S(1)}, u32[]{:S(2)}) copy-start(bf16[768]{0:T(1024)(128)(2,1)S(1)} %dynamic-update-slice.7) | copy-start | bytes 4612
  298.7 3.9 copy-start.71
  298.8 4.8 copy-start.63
  298.8 5.8 copy-start.74
  298.8 29.8 %copy-start.14 = (f32[256,768]{1,0:T(8,128)S(1)}, f32[256,768]{1,0:T(8,128)}, u32[]{:S(2)}) copy-start(f32[256,768]{1,0:T(8,128)} %copy-done.13) | copy-start | bytes 2359300
  302.6 28.6 %copy-start.8 = (bf16[256,3072]{1,0:T(8,128)(2,1)S(1)}, bf16[256,3072]{1,0:T(8,128)(2,1)}, u32[]{:S(2)}) copy-start(bf16[256,3072]{1,0:T(8,128)(2,1)} %copy-done.7) | copy-start | bytes 4718596
  302.6 28.6 %copy-start.12 = (f32[256,768]{1,0:T(8,128)S(1)}, f32[256,768]{1,0:T(8,128)}, u32[]{:S(2)}) copy-start(f32[256,768]{1,0:T(8,128)} %copy-done.9) | copy-start | bytes 2359300
  331.2 110.8 %copy-start.42 = (bf16[192,768]{1,0:T(8,128)(2,1)S(1)}, bf16[192,768]{1,0:T(8,128)(2,1)}, u32[]{:S(2)}) copy-start(bf16[192,768]{1,0:T(8,128)(2,1)} %reduce-scatter.10.cloned.1.call-done) | copy-start | bytes 884740
  331.2 110.8 %copy-start.78 = (f32[192]{0:T(256)S(1)}, f32[192]{0:T(256)}, u32[]{:S(2)}) copy-start(f32[192]{0:T(256)} %dynamic-slice_convert_fusion.8) | copy-start | bytes 2308
  331.2 110.8 %copy-start.79 = (f32[192]{0:T(256)S(1)}, f32[192]{0:T(256)}, u32[]{:S(2)}) copy-start(f32[192]{0:T(256)} %dynamic-slice_convert_fusion.7) | copy-start | bytes 2308
  331.3 110.7 %copy-start.80 = (f32[192]{0:T(256)S(1)}, f32[192]{0:T(256)}, u32[]{:S(2)}) copy-start(f32[192]{0:T(256)} %dynamic-slice_convert_fusion.6) | copy-start | bytes 2308
  331.3 110.7 %copy-start.81 = (f32[192]{0:T(256)S(1)}, f32[192]{0:T(256)}, u32[]{:S(2)}) copy-start(f32[192]{0:T(256)} %dynamic-slice_convert_fusion.5) | copy-start | bytes 2308
  331.3 110.7 %copy-start.82 = (f32[192]{0:T(256)S(1)}, f32[192]{0:T(256)}, u32[]{:S(2)}) copy-start(f32[192]{0:T(256)} %dynamic-slice_convert_fusion.4) | copy-start | bytes 2308
  331.3 110.7 %copy-start.83 = (f32[192]{0:T(256)S(1)}, f32[192]{0:T(256)}, u32[]{:S(2)}) copy-start(f32[192]{0:T(256)} %dynamic-slice_convert_fusion.3) | copy-start | bytes 2308
  331.3 110.7 %copy-start.84 = (f32[192]{0:T(256)S(1)}, f32[192]{0:T(256)}, u32[]{:S(2)}) copy-start(f32[192]{0:T(256)} %dynamic-slice_convert_fusion.2) | copy-start | bytes 2308
  331.3 110.7 %copy-start.85 = (f32[192]{0:T(256)S(1)}, f32[192]{0:T(256)}, u32[]{:S(2)}) copy-start(f32[192]{0:T(256)} %dynamic-slice_convert_fusion.1) | copy-start | bytes 2308
  (44 other events, 81.4 us)
Sparse Core Ops, SparseCore 0:
  10.2 33.4 all-gather.6
  48.2 28.6 all-gather.8
  78.4 17.4 all-gather.10
  97.9 37.4 all-gather.12
  137.4 37.4 all-gather.14
  231.6 37.9 reduce-scatter.5
  272.3 25.6 reduce-scatter.9
  300.6 47.8 reduce-scatter.11
  351.2 47.8 reduce-scatter.13
  401.5 40.4 reduce-scatter.7
where the time goes:
time: 737 us; the launch traced here: 728 us
  blocking collectives  309 us (42%)
  waiting for transfers between devices  244 us (33%)
  matrix products  74.1 us (10%)
  other arithmetic  44.7 us (6%)
  local copies, waits for them, and re-layouts  37.9 us (5%)
  between operations  18.4 us (2%)
    psum x1, blocking collectives, local(): lax.psum((sum_gain_one, sum_shift_one, sum_qkv, sum_bias_query, sum_bias_...  279 us
    reduce_scatter x1, waiting for transfers between devices, local(): lax.psum_scatter(grad_down.astype(jnp.bfloat16), 'shard', scatter_dimensi...  50.6 us
    reduce_scatter x1, waiting for transfers between devices, local(): lax.psum_scatter(grad_qkv.astype(jnp.bfloat16), 'shard', scatter_dimensio...  42.9 us
    all_gather x1, waiting for transfers between devices, local(): lax.all_gather(fc1_weight.astype(brain), 'shard', axis=0, tiled=True)  34.5 us
    all_gather x1, waiting for transfers between devices, local(): lax.all_gather(fc2_weight.astype(brain), 'shard', axis=0, tiled=True)  33.8 us
    unnamed x2, blocking collectives  24.6 us
    reduce_scatter x1, waiting for transfers between devices, local(): lax.psum_scatter(grad_weight_out.astype(jnp.bfloat16), 'shard', scatter_d...  21.2 us
    dot_general x4, matrix products, multiply_by_transpose(): lax.dot_general(left, right, (((1,), (1,)), ((), ())), preferred_element_...  19.1 us
  transfers between devices with their start and end apart: 10, of which 10 were waited for; matrix products, arithmetic and copies ran while one was open for 12% of the time, Pallas kernels for 0%

commit v1 on v0

v1 whole, which is shorter than its diff:
```python
import functools

import jax
import jax.numpy as jnp
from jax import lax
from jax.experimental import pallas as pl
from jax.experimental.pallas import tpu as pltpu
from jax.sharding import PartitionSpec as P

D = 768
HD = 64
EPSILON = 1e-06
GROUP = 4
SLICE = D // GROUP
LOCAL_HEADS = SLICE // HD
HALF = D // 2
MIDDLE = 4
PIECE = SLICE // MIDDLE
BRAIN = jnp.bfloat16
SINGLE = jnp.float32
MESH = pl.DeviceIdType.MESH

G1, B1, BO, G2, B2, C2, BQ, BV, C1 = range(9)
VECTOR_ROWS = 16


class Names:
    def __init__(self):
        self.total = 0

    def take(self, count):
        first = self.total
        self.total += count
        return first


ids = Names()
ID_TOKENS = ids.take(3)
ID_COTANGENT = ids.take(3)
ID_GRADIENT = ids.take(3)
ID_VECTORS = ids.take(3)
ID_QKV = ids.take(3)
ID_OUT = ids.take(3)
ID_UP = ids.take(3)
ID_MIX = ids.take(6)
ID_SUM_TWO = ids.take(3)
ID_SUM_RESULT = ids.take(3)
ID_SUM_ONE = ids.take(3)
ID_SMALL = ids.take(3)
ID_WEIGHTS = ids.take(4 * 16)
COPIES = ids.total
LOCALS = 16


def to_single(value):
    return value.astype(SINGLE)


def dot(left, right, left_dim, right_dim):
    return lax.dot_general(
        left, right, (((left_dim,), (right_dim,)), ((), ())), preferred_element_type=SINGLE
    )


def normalize(value):
    mean = jnp.sum(value, axis=-1, keepdims=True) * (1.0 / D)
    centred = value - mean
    spread = jnp.sum(centred * centred, axis=-1, keepdims=True) * (1.0 / D)
    scale = lax.rsqrt(spread + EPSILON)
    return centred * scale, scale


def norm_back(grad, normal, scale, gain):
    scaled = grad * gain
    first = jnp.sum(scaled, axis=-1, keepdims=True) * (1.0 / D)
    second = jnp.sum(scaled * normal, axis=-1, keepdims=True) * (1.0 / D)
    return scale * (scaled - first - normal * second)


def row_sum(value):
    return jnp.sum(value, axis=0, keepdims=True)


def kernel(
    replicas,
    tokens_in,
    cotangent_in,
    count_in,
    vectors_in,
    qkv_in,
    out_in,
    up_in,
    down_in,
    outputs_out,
    input_grad_out,
    vectors_out,
    qkv_out,
    out_out,
    up_out,
    down_out,
    qkv_wide,
    out_wide,
    up_wide,
    down_wide,
    qkv_cut,
    up_cut,
    qkv_own,
    up_own,
    out_all,
    down_own,
    vectors,
    tokens,
    cotangent,
    hidden_one,
    pairs,
    soft,
    mixed,
    middle_own,
    hidden_two,
    active,
    lifted_grad,
    gradient,
    middle_grad,
    mixed_grad,
    pairs_grad,
    sum_sent,
    sum_near,
    sum_far,
    sum_own,
    out_grad,
    qkv_grad,
    y_down,
    y_up,
    y_out,
    y_qkv,
    z_down,
    z_up,
    z_out,
    z_qkv,
    piece_down,
    piece_up,
    piece_out,
    piece_qkv,
    cross_up,
    cross_qkv,
    full_down,
    full_up,
    full_out,
    full_qkv,
    columns,
    small_sent,
    small_near,
    small_all,
    result_stage,
    *rest,
):
    outer = replicas // (2 * MIDDLE)
    if outer > 1:
        outer_down, outer_up, outer_out, outer_qkv, send, recv, send_all, recv_all, near = rest
    else:
        send, recv, send_all, recv_all, near = rest
    rows = tokens_in.shape[0]
    slot = rows // 2
    group_rows = rows * GROUP

    shard = lax.axis_index("shard")
    replica = lax.axis_index("replica")
    y = replica % 2
    z = (replica // 2) % MIDDLE
    far = replica // (2 * MIDDLE)
    y_peer = replica + 1 - 2 * y

    def mate(step):
        return 2 * ((shard // 2 + step // 2) % 2) + (shard + step) % 2

    def z_at(step):
        return (z + step) % MIDDLE

    def z_peer(step):
        return replica + 2 * (z_at(step) - z)

    finals = []

    def remote(source, target, index, **where):
        return pltpu.make_async_remote_copy(
            src_ref=source,
            dst_ref=target,
            send_sem=send.at[index],
            recv_sem=recv.at[index],
            device_id=where,
            device_id_type=MESH,
        )

    def push(make):
        make().start()
        finals.append(make)

    def local(source, target, index):
        return pltpu.make_async_copy(source, target, near.at[index])

    def block(index, size):
        return pl.ds(pl.multiple_of(index * size, size), size)

    loads = [
        local(tokens_in, tokens.at[block(shard, rows)], 0),
        local(vectors_in, vectors.at[shard], 1),
        local(qkv_in, qkv_wide, 2),
        local(cotangent_in, cotangent.at[block(shard, rows)], 3),
        local(up_in, up_wide, 4),
        local(out_in, out_wide, 5),
        local(down_in, down_wide, 6),
    ]
    for load in loads:
        load.start()
    barrier = pltpu.get_barrier_semaphore()
    for step in (1, 2, 3):
        pl.semaphore_signal(barrier, inc=1, device_id={"shard": mate(step)}, device_id_type=MESH)

    def greet(step, carry):
        peer = (replica + step) % replicas
        pl.semaphore_signal(barrier, inc=1, device_id={"replica": peer}, device_id_type=MESH)
        return carry

    lax.fori_loop(1, replicas, greet, 0)
    loads[0].wait()
    loads[1].wait()
    pl.semaphore_wait(barrier, replicas + 2)

    def gather_near(buffer, base):
        return remote(
            buffer.at[block(shard, rows)], buffer.at[block(shard, rows)], base, shard=mate(1)
        )

    def gather_across(buffer, base):
        return remote(
            buffer.at[block(shard, rows)], buffer.at[block(shard, rows)], base + 1, shard=mate(2)
        )

    def gather_on(buffer, base):
        there = block(mate(2), rows)
        return remote(buffer.at[there], buffer.at[there], base + 2, shard=mate(1))

    def gather_start(buffer, base):
        push(functools.partial(gather_across, buffer, base))
        push(functools.partial(gather_near, buffer, base))

    def gather_forward(buffer, base):
        gather_across(buffer, base).wait_recv()
        push(functools.partial(gather_on, buffer, base))

    def gather_wait(buffer, base, step):
        @pl.when(step == 1)
        def _():
            gather_near(buffer, base).wait_recv()

        @pl.when(step == 3)
        def _():
            gather_on(buffer, base).wait_recv()

    gather_start(tokens, ID_TOKENS)
    for step in (1, 2, 3):
        push(
            functools.partial(
                lambda step: remote(
                    vectors.at[shard],
                    vectors.at[shard],
                    ID_VECTORS + step - 1,
                    shard=mate(step),
                ),
                step,
            )
        )

    loads[2].wait()
    for member in range(GROUP):
        left = member * SLICE
        qkv_cut[member] = jnp.concatenate(
            [
                qkv_wide[:, part * D + left : part * D + left + SLICE].astype(BRAIN)
                for part in range(3)
            ],
            axis=1,
        )

    def send_qkv(step):
        return remote(
            qkv_cut.at[mate(step)],
            qkv_own.at[block(shard, SLICE)],
            ID_QKV + step - 1,
            shard=mate(step),
        )

    def send_up(step):
        return remote(
            up_cut.at[mate(step)],
            up_own.at[block(shard, SLICE)],
            ID_UP + step - 1,
            shard=mate(step),
        )

    def send_out(step):
        here = block(shard, SLICE)
        return remote(out_all.at[here], out_all.at[here], ID_OUT + step - 1, shard=mate(step))

    for step in (2, 3, 1):
        push(functools.partial(send_qkv, step))
    qkv_own[block(shard, SLICE), :] = qkv_cut[shard]
    loads[3].wait()
    loads[4].wait()
    loads[5].wait()
    loads[6].wait()
    second_live = to_single(jnp.minimum(count_in[0] - 1, 1))
    live_rows = jnp.where(
        lax.broadcasted_iota(jnp.int32, (rows, 1), 0) < slot, 1.0, second_live
    )
    own = block(shard, rows)
    cotangent[own, :] = (to_single(cotangent[own, :]) * live_rows).astype(BRAIN)
    out_all[block(shard, SLICE), :] = out_wide[...].astype(BRAIN)
    for member in range(GROUP):
        up_cut[member] = up_wide[:, member * D : (member + 1) * D].astype(BRAIN)
    up_own[block(shard, SLICE), :] = up_cut[shard]
    down_own[...] = down_wide[...].astype(BRAIN)
    columns[...] = jnp.zeros_like(columns)
    pairs_grad[...] = jnp.zeros_like(pairs_grad)

    gather_forward(tokens, ID_TOKENS)
    for step in (1, 2, 3):
        remote(
            vectors.at[shard], vectors.at[mate(step)], ID_VECTORS + step - 1, shard=mate(step)
        ).wait_recv()
    for step in (1, 2, 3):
        send_qkv(step).wait_recv()

    for step in (2, 3, 1):
        push(functools.partial(send_out, step))
    for step in (2, 3, 1):
        push(functools.partial(send_up, step))
    gather_start(cotangent, ID_COTANGENT)

    def whole(row):
        return jnp.concatenate([vectors[member, row : row + 1, :] for member in range(GROUP)], 1)

    def mine(row):
        return vectors[shard, row : row + 1, :]

    scale_row = jnp.where(
        lax.broadcasted_iota(jnp.int32, (1, 3 * SLICE), 1) < SLICE, HD**-0.5, 1.0
    )

    def project(step, carry):
        gather_wait(tokens, ID_TOKENS, step)
        here = block(mate(step), rows)
        normal, _ = normalize(to_single(tokens[here, :]))
        hidden = (normal * whole(G1) + whole(B1)).astype(BRAIN)
        hidden_one[here, :] = hidden
        bias = jnp.concatenate([mine(BQ), jnp.zeros((1, SLICE), SINGLE), mine(BV)], 1)
        product = (dot(hidden, qkv_own[...], 1, 0) + bias) * scale_row
        pairs[here, :] = product.astype(BRAIN)
        return carry

    lax.fori_loop(0, GROUP, project, 0)

    def clip_rows(ref, clip, left):
        return jnp.concatenate(
            [
                ref[pl.ds(pl.multiple_of(member * rows + clip * slot, slot), slot), left : left + HD]
                for member in range(GROUP)
            ],
            0,
        )

    def mixed_part(owner, clip):
        return mixed.at[owner, :, pl.ds(pl.multiple_of(clip * slot, slot), slot), :]

    def mix_near(clip):
        return remote(
            mixed_part(shard, clip), mixed_part(shard, clip), ID_MIX + clip, shard=mate(1)
        )

    def mix_across(clip):
        return remote(
            mixed_part(shard, clip), mixed_part(shard, clip), ID_MIX + 2 + clip, shard=mate(2)
        )

    def mix_on(clip):
        return remote(
            mixed_part(mate(2), clip), mixed_part(mate(2), clip), ID_MIX + 4 + clip, shard=mate(1)
        )

    def attend(clip, carry):
        for head in range(LOCAL_HEADS):
            query = clip_rows(pairs, clip, head * HD)
            key = clip_rows(pairs, clip, SLICE + head * HD)
            value = clip_rows(pairs, clip, 2 * SLICE + head * HD)
            scores = dot(key, query, 1, 1)
            highest = jnp.max(scores, axis=0, keepdims=True)
            expanded = jnp.exp(scores - highest)
            softened = expanded * (1.0 / row_sum(expanded))
            soft[clip * LOCAL_HEADS + head] = softened
            mixture = dot(value.T, softened.astype(BRAIN), 1, 0).T.astype(BRAIN)
            for member in range(GROUP):
                mixed[
                    shard,
                    member,
                    pl.ds(pl.multiple_of(clip * slot, slot), slot),
                    head * HD : (head + 1) * HD,
                ] = mixture[member * slot : (member + 1) * slot]
        mix_across(clip).start()
        mix_near(clip).start()
        return carry

    lax.fori_loop(0, 2, attend, 0)
    gather_forward(cotangent, ID_COTANGENT)
    for clip in (0, 1):
        finals.append(functools.partial(mix_near, clip))
        finals.append(functools.partial(mix_across, clip))
        mix_across(clip).wait_recv()
        push(functools.partial(mix_on, clip))
    for step in (1, 2, 3):
        send_out(step).wait_recv()
        send_up(step).wait_recv()
    gather_near(cotangent, ID_COTANGENT).wait_recv()
    gather_on(cotangent, ID_COTANGENT).wait_recv()
    for clip in (0, 1):
        mix_near(clip).wait_recv()
        mix_on(clip).wait_recv()

    def sum_near_copy(which, base, part):
        return remote(
            sum_sent.at[which, part], sum_near.at[which, part], base + part, shard=mate(1)
        )

    def sum_far_copy(which, base):
        return remote(sum_sent.at[which, 2], sum_far.at[which], base + 2, shard=mate(2))

    def sum_step(which, base, step, value):
        sum_own[which] = value

        @pl.when(step == 0)
        def _():
            sum_sent[which, 0] = sum_own[which].astype(BRAIN)
            sum_near_copy(which, base, 0).start()

        @pl.when(step == 1)
        def _():
            sum_near_copy(which, base, 0).wait_recv()
            sum_sent[which, 2] = (sum_own[which] + to_single(sum_near[which, 0])).astype(BRAIN)
            sum_far_copy(which, base).start()

        @pl.when(step == 2)
        def _():
            sum_sent[which, 1] = sum_own[which].astype(BRAIN)
            sum_near_copy(which, base, 1).start()

    def sum_end(which, base):
        sum_near_copy(which, base, 0).wait_send()
        sum_near_copy(which, base, 1).wait()
        sum_far_copy(which, base).wait()
        return sum_own[which] + to_single(sum_near[which, 1]) + to_single(sum_far[which])

    def feed(step, carry):
        chunk = mate(3 - step)
        here = block(chunk, rows)
        total = to_single(tokens[here, :]) + whole(BO)
        for member in range(GROUP):
            total += dot(
                mixed[member, chunk], out_all[member * SLICE : (member + 1) * SLICE, :], 1, 0
            )

        @pl.when(step == 3)
        def _():
            middle_own[...] = total

        normal, _ = normalize(total)
        hidden = (normal * whole(G2) + whole(B2)).astype(BRAIN)
        hidden_two[here, :] = hidden
        bias = jnp.concatenate(
            [vectors[shard, C1 + part : C1 + part + 1, :] for part in range(GROUP)], 1
        )
        lifted = dot(hidden, up_own[...], 1, 0) + bias
        share = 0.5 + 0.5 * lax.erf(lifted * (0.5**0.5))
        active[here, :] = (lifted * share).astype(BRAIN)
        slope = share + lifted * jnp.exp(lifted * lifted * -0.5) * 0.3989422804014327
        down = cotangent[here, :]
        columns[0:1, :] += row_sum(to_single(down))
        grad = (dot(down, down_own[...], 1, 1) * slope).astype(BRAIN)
        lifted_grad[here, :] = grad
        columns[1:2, :] += row_sum(to_single(grad))
        sum_step(0, ID_SUM_TWO, step, dot(grad, up_own[...], 1, 1))
        return carry

    lax.fori_loop(0, GROUP, feed, 0)

    stages = {}

    def weight(name, number, grad, halves, quarters, piece, crossed, full, outers):
        base = ID_WEIGHTS + 16 * number
        blocks = piece.shape[0]
        my_half = pl.ds(pl.multiple_of(y * HALF, HALF), HALF)
        their_half = pl.ds(pl.multiple_of((1 - y) * HALF, HALF), HALF)
        source = piece if crossed is None else crossed

        def piece_rows(step):
            return pl.ds(pl.multiple_of(z_at(step) * PIECE, PIECE), PIECE)

        def y_copy():
            return remote(grad.at[:, :, their_half], halves, base, replica=y_peer)

        def z_copy(step):
            return remote(
                halves.at[:, piece_rows(step), :],
                quarters.at[step - 1],
                base + step,
                replica=z_peer(step),
            )

        def cross_copy(step):
            return remote(
                piece.at[mate(step)], crossed.at[shard], base + 3 + step, shard=mate(step)
            )

        def z_back(step):
            return remote(
                source,
                full.at[y, :, piece_rows(0), :],
                base + 6 + step,
                replica=z_peer(step),
            )

        def y_back(step):
            part = full.at[y, :, piece_rows(-step + MIDDLE), :]
            return remote(part, part, base + 10 + step, replica=y_peer)

        def y_start():
            push(y_copy)

        def z_start():
            y_copy().wait_recv()
            for index in range(blocks):
                halves[index] = (
                    to_single(grad[index, :, my_half]) + to_single(halves[index])
                ).astype(BRAIN)
            for step in (2, 1, 3):
                push(functools.partial(z_copy, step))

        def outer_start():
            for step in (1, 2, 3):
                z_copy(step).wait_recv()
            for index in range(blocks):
                total = to_single(halves[index, piece_rows(0), :])
                for step in (1, 2, 3):
                    total += to_single(quarters[step - 1, index])
                piece[index] = total.astype(BRAIN)
            if outers is not None:
                outers[far] = piece[...]

                def outer_copy(step):
                    return pltpu.make_async_remote_copy(
                        src_ref=piece,
                        dst_ref=outers.at[far],
                        send_sem=send_all.at[number + 1, step],
                        recv_sem=recv_all.at[number + 1, step],
                        device_id={
                            "replica": replica
                            + 2 * MIDDLE * ((far + step) % outer - far)
                        },
                        device_id_type=MESH,
                    )

                for step in range(1, outer):
                    outer_copy(step).start()
                for step in range(1, outer):
                    outer_copy(step).wait()
                total = to_single(outers[0])
                for step in range(1, outer):
                    total += to_single(outers[step])
                piece[...] = total.astype(BRAIN)
            if crossed is not None:
                crossed[shard] = piece[shard]
                for step in (2, 3, 1):
                    push(functools.partial(cross_copy, step))

        def back_start():
            if crossed is not None:
                for step in (1, 2, 3):
                    cross_copy(step).wait_recv()
            for step in (2, 1, 3):
                push(functools.partial(z_back, step))
            for index in range(blocks):
                full[y, index, piece_rows(0), :] = source[index]
            push(functools.partial(y_back, 0))

        def back_on():
            for step in (1, 3, 2):
                z_back(step).wait_recv()
                push(functools.partial(y_back, step))

        def back_end():
            for step in range(MIDDLE):
                y_back(step).wait_recv()

        stages[name] = (y_start, z_start, outer_start, back_start, back_on, back_end)

    weight(
        "down", 0, up_cut, y_down, z_down, piece_down, None, full_down,
        outer_down if outer > 1 else None,
    )
    weight(
        "up", 1, qkv_grad.at[1], y_up, z_up, piece_up, cross_up, full_up,
        outer_up if outer > 1 else None,
    )
    weight(
        "out", 2, out_grad, y_out, z_out, piece_out, None, full_out,
        outer_out if outer > 1 else None,
    )
    weight(
        "qkv", 3, qkv_grad.at[0], y_qkv, z_qkv, piece_qkv, cross_qkv, full_qkv,
        outer_qkv if outer > 1 else None,
    )

    def run(name, stage):
        stages[name][stage]()

    for step in (1, 2, 3):
        send_up(step).wait_send()
    finals[:] = [item for item in finals if getattr(item, "func", None) is not send_up]

    def cut_product(target, left, right, width):
        for part in range(2):
            product = dot(left[:, part * HALF : (part + 1) * HALF], right[...], 0, 0)
            for half in range(2):
                target[2 * part + half, :, 0:width] = product[
                    half * SLICE : (half + 1) * SLICE
                ].astype(BRAIN)

    cut_product(up_cut, active, cotangent, D)
    run("down", 0)
    cut_product(qkv_grad.at[1], hidden_two, lifted_grad, D)
    run("up", 0)

    grad_two = sum_end(0, ID_SUM_TWO)
    normal, scale = normalize(middle_own[...])
    own_cotangent = to_single(cotangent[own, :])
    small_sent_rows = [row_sum(grad_two * normal), row_sum(grad_two)]
    total = own_cotangent + norm_back(grad_two, normal, scale, whole(G2))
    middle_grad[...] = total
    gradient[own, :] = total.astype(BRAIN)
    gather_start(gradient, ID_GRADIENT)
    columns[2:3, :] = small_sent_rows[0]
    columns[3:4, :] = small_sent_rows[1]

    def lower(step, carry):
        here = block(mate(3 - step), rows)
        sum_step(1, ID_SUM_RESULT, step, dot(active[here, :], down_own[...], 1, 0))
        return carry

    lax.fori_loop(0, GROUP, lower, 0)
    run("down", 1)
    gather_forward(gradient, ID_GRADIENT)
    run("up", 1)

    def back_out(step, carry):
        gather_wait(gradient, ID_GRADIENT, step)
        chunk = mate(step)
        grad = gradient[block(chunk, rows), :]
        columns[4:5, :] += row_sum(to_single(grad))
        mixed_grad[block(chunk, rows), :] = dot(
            grad, out_all[block(shard, SLICE), :], 1, 1
        ).astype(BRAIN)
        return carry

    lax.fori_loop(0, GROUP, back_out, 0)
    out_grad[0] = dot(mixed[shard].reshape(group_rows, SLICE), gradient[...], 0, 0).astype(BRAIN)
    run("out", 0)
    result = (
        middle_own[...] + sum_end(1, ID_SUM_RESULT) + whole(C2)
    ) * live_rows
    result_stage[...] = result.astype(BRAIN)
    result_copy = local(result_stage, outputs_out, 7)
    result_copy.start()

    def attend_back(clip, carry):
        for head in range(LOCAL_HEADS):
            query = clip_rows(pairs, clip, head * HD)
            key = clip_rows(pairs, clip, SLICE + head * HD)
            value = clip_rows(pairs, clip, 2 * SLICE + head * HD)
            grad = clip_rows(mixed_grad, clip, head * HD)
            softened = soft[clip * LOCAL_HEADS + head]
            grad_soft = dot(value, grad, 1, 1)
            inner = row_sum(grad_soft * softened)
            grad_scores = (softened * (grad_soft - inner)).astype(BRAIN)
            parts = (
                (dot(key.T, grad_scores, 1, 0).T * HD**-0.5).astype(BRAIN),
                dot(grad_scores, query, 1, 0).astype(BRAIN),
                dot(softened.astype(BRAIN), grad, 1, 0).astype(BRAIN),
            )
            for part, entry in enumerate(parts):
                left = part * SLICE + head * HD
                for member in range(GROUP):
                    pairs_grad[
                        pl.ds(pl.multiple_of(member * rows + clip * slot, slot), slot),
                        left : left + HD,
                    ] = entry[member * slot : (member + 1) * slot]
        return carry

    attend_back(0, 0)
    run("down", 2)
    run("up", 2)
    run("out", 1)
    attend_back(1, 0)
    run("down", 3)
    run("up", 3)

    cut_product(qkv_grad.at[0], hidden_one, pairs_grad, 3 * SLICE)
    qkv_grad[0, :, :, 3 * SLICE :] = jnp.zeros((GROUP, SLICE, SLICE), BRAIN)
    run("qkv", 0)

    def back_project(step, carry):
        here = block(mate(3 - step), rows)
        grad = pairs_grad[here, :]
        columns[5:6, 0 : 3 * SLICE] += row_sum(to_single(grad))
        sum_step(0, ID_SUM_ONE, step, dot(grad, qkv_own[...], 1, 1))
        return carry

    lax.fori_loop(0, GROUP, back_project, 0)
    run("out", 2)
    run("down", 4)
    run("up", 4)
    run("qkv", 1)
    run("out", 3)

    grad_one = sum_end(0, ID_SUM_ONE)
    normal, scale = normalize(to_single(tokens[own, :]))
    columns[6:7, :] = row_sum(grad_one * normal)
    columns[7:8, :] = row_sum(grad_one)
    middle_grad[...] += norm_back(grad_one, normal, scale, whole(G1))
    grad_copy = local(middle_grad, input_grad_out, 8)
    grad_copy.start()

    for member in range(GROUP):
        at = slice(member * SLICE, (member + 1) * SLICE)
        for place, row in enumerate((6, 7, 2, 3, 4, 0)):
            small_sent[member, place : place + 1, :] = columns[row : row + 1, at]

    def small_copy(step):
        return remote(
            small_sent.at[mate(step)], small_near.at[step - 1], ID_SMALL + step - 1, shard=mate(step)
        )

    for step in (1, 2, 3):
        push(functools.partial(small_copy, step))
    run("qkv", 2)
    run("out", 4)
    for step in (1, 2, 3):
        small_copy(step).wait_recv()
    summed = (
        small_sent[shard, 0:4, :] + small_near[0, 0:4, :] + small_near[1, 0:4, :] + small_near[2, 0:4, :]
    )
    small_all[replica, G1 : G1 + 2, :] = summed[0:2]
    small_all[replica, G2 : G2 + 2, :] = summed[2:4]
    small_all[replica, BO : BO + 1, :] = small_sent[shard, 4:5, :]
    small_all[replica, C2 : C2 + 1, :] = small_sent[shard, 5:6, :]
    small_all[replica, BQ : BQ + 1, :] = columns[5:6, 0:SLICE]
    small_all[replica, BV : BV + 1, :] = columns[5:6, 2 * SLICE : 3 * SLICE]
    for part in range(GROUP):
        small_all[replica, C1 + part : C1 + part + 1, :] = columns[
            1:2, part * SLICE : (part + 1) * SLICE
        ]
    small_all[replica, C1 + GROUP :, :] = jnp.zeros((VECTOR_ROWS - C1 - GROUP, SLICE), SINGLE)

    def spread_copy(step):
        return pltpu.make_async_remote_copy(
            src_ref=small_all.at[replica],
            dst_ref=small_all.at[replica],
            send_sem=send_all.at[0, step],
            recv_sem=recv_all.at[0, step],
            device_id={"replica": (replica + step) % replicas},
            device_id_type=MESH,
        )

    def spread_start(step, carry):
        spread_copy(step).start()
        return carry

    lax.fori_loop(1, replicas, spread_start, 0)

    run("down", 5)
    for index in range(GROUP):
        for half in range(2):
            down_wide[
                index * SLICE : (index + 1) * SLICE, half * HALF : (half + 1) * HALF
            ] = to_single(full_down[half, index])
    down_copy = local(down_wide, down_out, 9)
    down_copy.start()
    run("up", 5)
    for index in range(GROUP):
        for half in range(2):
            left = index * D + half * HALF
            up_wide[:, left : left + HALF] = to_single(full_up[half, index])
    up_copy = local(up_wide, up_out, 10)
    up_copy.start()
    run("qkv", 3)
    run("out", 5)
    for half in range(2):
        out_wide[:, half * HALF : (half + 1) * HALF] = to_single(full_out[half, 0])
    out_copy = local(out_wide, out_out, 11)
    out_copy.start()
    run("qkv", 4)

    def spread_wait(step, carry):
        spread_copy(step).wait()
        return carry

    lax.fori_loop(1, replicas, spread_wait, 0)
    small_sum = small_all[0]
    for step in range(1, replicas):
        small_sum += small_all[step]
    small_all[0] = small_sum
    vectors_copy = local(small_all.at[0], vectors_out, 12)
    vectors_copy.start()
    run("qkv", 5)
    for part in range(3):
        half, left = ((0, 0), (0, SLICE), (1, 0))[part]
        qkv_wide[:, part * D : (part + 1) * D] = to_single(
            jnp.concatenate(
                [full_qkv[half, index, :, left : left + SLICE] for index in range(GROUP)], 1
            )
        )
    qkv_copy = local(qkv_wide, qkv_out, 13)
    qkv_copy.start()
    for item in finals:
        item().wait_send()
    for item in (result_copy, grad_copy, down_copy, up_copy, out_copy, vectors_copy, qkv_copy):
        item.wait()


def local(replicas, *arguments):
    (
        tokens, cotangent, clip_count, ln1_gain, ln1_bias, qkv_weight, q_bias, v_bias,
        out_weight, out_bias, ln2_gain, ln2_bias, fc1_weight, fc1_bias, fc2_weight, fc2_bias,
    ) = arguments
    slots, local_tokens, _ = tokens.shape
    rows = slots * local_tokens
    group_rows = rows * GROUP
    outer = replicas // (2 * MIDDLE)
    table = jnp.stack(
        [ln1_gain, ln1_bias, out_bias, ln2_gain, ln2_bias, fc2_bias, q_bias, v_bias]
        + [fc1_bias[part * SLICE : (part + 1) * SLICE] for part in range(GROUP)]
        + [jnp.zeros_like(ln1_gain)] * (VECTOR_ROWS - C1 - GROUP)
    )
    table = table.astype(BRAIN).astype(SINGLE)
    counts = (GROUP, GROUP, 1, GROUP)
    scratch = [
        pltpu.VMEM((SLICE, 3 * D), SINGLE),
        pltpu.VMEM((SLICE, D), SINGLE),
        pltpu.VMEM((SLICE, 4 * D), SINGLE),
        pltpu.VMEM((D, D), SINGLE),
        pltpu.VMEM((GROUP, SLICE, 3 * SLICE), BRAIN),
        pltpu.VMEM((GROUP, SLICE, D), BRAIN),
        pltpu.VMEM((D, 3 * SLICE), BRAIN),
        pltpu.VMEM((D, D), BRAIN),
        pltpu.VMEM((D, D), BRAIN),
        pltpu.VMEM((D, D), BRAIN),
        pltpu.VMEM((GROUP, VECTOR_ROWS, SLICE), SINGLE),
        pltpu.VMEM((group_rows, D), BRAIN),
        pltpu.VMEM((group_rows, D), BRAIN),
        pltpu.VMEM((group_rows, D), BRAIN),
        pltpu.VMEM((group_rows, 3 * SLICE), BRAIN),
        pltpu.VMEM((2 * LOCAL_HEADS, group_rows // 2, group_rows // 2), SINGLE),
        pltpu.VMEM((GROUP, GROUP, rows, SLICE), BRAIN),
        pltpu.VMEM((rows, D), SINGLE),
        pltpu.VMEM((group_rows, D), BRAIN),
        pltpu.VMEM((group_rows, D), BRAIN),
        pltpu.VMEM((group_rows, D), BRAIN),
        pltpu.VMEM((group_rows, D), BRAIN),
        pltpu.VMEM((rows, D), SINGLE),
        pltpu.VMEM((group_rows, SLICE), BRAIN),
        pltpu.VMEM((group_rows, 3 * SLICE), BRAIN),
        pltpu.VMEM((2, 3, rows, D), BRAIN),
        pltpu.VMEM((2, 2, rows, D), BRAIN),
        pltpu.VMEM((2, rows, D), BRAIN),
        pltpu.VMEM((2, rows, D), SINGLE),
        pltpu.VMEM((1, SLICE, D), BRAIN),
        pltpu.VMEM((2, GROUP, SLICE, D), BRAIN),
    ]
    scratch += [pltpu.VMEM((count, SLICE, HALF), BRAIN) for count in counts]
    scratch += [pltpu.VMEM((MIDDLE - 1, count, PIECE, HALF), BRAIN) for count in counts]
    scratch += [pltpu.VMEM((count, PIECE, HALF), BRAIN) for count in counts]
    scratch += [pltpu.VMEM((GROUP, PIECE, HALF), BRAIN) for _ in range(2)]
    scratch += [pltpu.VMEM((2, count, SLICE, HALF), BRAIN) for count in counts]
    scratch += [
        pltpu.VMEM((8, D), SINGLE),
        pltpu.VMEM((GROUP, 8, SLICE), SINGLE),
        pltpu.VMEM((GROUP - 1, 8, SLICE), SINGLE),
        pltpu.VMEM((replicas, VECTOR_ROWS, SLICE), SINGLE),
        pltpu.VMEM((rows, D), BRAIN),
    ]
    if outer > 1:
        scratch += [pltpu.VMEM((outer, count, PIECE, HALF), BRAIN) for count in counts]
    scratch += [
        pltpu.SemaphoreType.DMA((COPIES,)),
        pltpu.SemaphoreType.DMA((COPIES,)),
        pltpu.SemaphoreType.DMA((5, replicas)),
        pltpu.SemaphoreType.DMA((5, replicas)),
        pltpu.SemaphoreType.DMA((LOCALS,)),
    ]
    anywhere = pl.BlockSpec(memory_space=pl.ANY)
    outputs, input_grad, small, qkv_grad, out_grad, up_grad, down_grad = pl.pallas_call(
        functools.partial(kernel, replicas),
        out_shape=(
            jax.ShapeDtypeStruct((rows, D), BRAIN),
            jax.ShapeDtypeStruct((rows, D), SINGLE),
            jax.ShapeDtypeStruct((VECTOR_ROWS, SLICE), SINGLE),
            jax.ShapeDtypeStruct(qkv_weight.shape, SINGLE),
            jax.ShapeDtypeStruct(out_weight.shape, SINGLE),
            jax.ShapeDtypeStruct(fc1_weight.shape, SINGLE),
            jax.ShapeDtypeStruct(fc2_weight.shape, SINGLE),
        ),
        in_specs=[
            anywhere,
            anywhere,
            pl.BlockSpec(memory_space=pltpu.SMEM),
            anywhere,
            anywhere,
            anywhere,
            anywhere,
            anywhere,
        ],
        out_specs=(anywhere,) * 7,
        scratch_shapes=scratch,
        compiler_params=pltpu.CompilerParams(
            collective_id=0, has_side_effects=True, vmem_limit_bytes=65000 * 1024
        ),
        name="layer",
    )(
        tokens.reshape(rows, D),
        cotangent.reshape(rows, D),
        clip_count,
        table,
        qkv_weight,
        out_weight,
        fc1_weight,
        fc2_weight,
    )
    return (
        outputs.reshape(tokens.shape),
        input_grad.reshape(tokens.shape),
        small[G1],
        small[B1],
        qkv_grad,
        small[BQ],
        small[BV],
        out_grad,
        small[BO],
        small[G2],
        small[B2],
        up_grad,
        small[C1 : C1 + GROUP].reshape(-1),
        down_grad,
        small[C2],
    )


def solution(mesh):
    token, vector, matrix = P("replica", "shard", None), P("shard"), P("shard", None)
    return jax.shard_map(
        functools.partial(local, mesh.shape["replica"]),
        mesh=mesh,
        in_specs=(
            token, token, P("replica"), vector, vector, matrix, vector, vector,
            matrix, vector, vector, vector, matrix, vector, matrix, vector,
        ),
        out_specs=(
            token, token, vector, vector, matrix, vector, vector, matrix,
            vector, vector, vector, matrix, vector, matrix, vector,
        ),
        check_vma=False,
    )
```

time: 737 us -> 224 us (0.30)
  blocking collectives: 309 us -> 0 us
  waiting for transfers between devices: 244 us -> 0 us
  Pallas kernels: 0 us -> 199 us
  matrix products: 74.1 us -> 0 us
  other arithmetic: 44.7 us -> 6.75 us
  local copies, waits for them, and re-layouts: 37.9 us -> 13.6 us
  between operations: 18.4 us -> 1.34 us
    psum x1 -> x0, blocking collectives: 279 us -> none  [local(): lax.psum((sum_gain_one, sum_shift_one, sum_qkv, sum_bias_query, sum_bias_...]
    pallas_call x0 -> x1, Pallas kernels: none -> 199 us  [local(): pl.pallas_call(functools.partial(kernel, replicas), out_shape=(jax.ShapeD...]
    reduce_scatter x5 -> x0, waiting for transfers between devices: 142 us -> none  [the longest x1 50.6 us: local(): lax.psum_scatter(grad_down.astype(jnp.bfloat16), 'shard', scatter_dimensi...]
    all_gather x5 -> x0, waiting for transfers between devices: 101 us -> none  [the longest x1 34.5 us: local(): lax.all_gather(fc1_weight.astype(brain), 'shard', axis=0, tiled=True)]
    dot_general x24 -> x0, matrix products: 74.1 us -> none  [the longest x4 19.1 us: multiply_by_transpose(): lax.dot_general(left, right, (((1,), (1,)), ((), ())), preferred_element_...]
    convert_element_type x38 -> x1, other arithmetic: 31.1 us -> 0.61 us  [local(): table = table.astype(BRAIN).astype(SINGLE)]
    unnamed x2 -> x0, blocking collectives: 24.6 us -> none
    slice x12 -> x3, local copies, waits for them, and re-layouts: 12.7 us -> 2.49 us  [the longest x1 1.58 us: local(): small[C2]]
  transfers between devices with their start and end apart: 10 -> 0, of which waited for: 10 -> 0; matrix products, arithmetic and copies ran while one was open for 12% -> 0% of each run, Pallas kernels for 0% -> 0%
where the time goes in v1:
time: 224 us; the launch traced here: 220 us
  Pallas kernels  199 us (89%)
  local copies, waits for them, and re-layouts  13.6 us (6%)
  other arithmetic  6.75 us (3%)
    pallas_call x1, Pallas kernels, local(): pl.pallas_call(functools.partial(kernel, replicas), out_shape=(jax.ShapeD...  199 us
    unnamed x14, local copies, waits for them, and re-layouts  10.3 us
    another operation x9, other arithmetic  6.13 us

profile of v1, /device:TPU:0, one launch (start us, length us, event | category | flops | bytes accessed | tf_op | source)
XLA Modules:
  0.0 220.2 jit_solution(13859745069738830821)
XLA Ops:
  1.3 0.7 convert.48
  2.0 0.7 convert.49
  2.7 0.7 convert.54
  3.4 0.7 convert.55
  4.0 0.7 convert.50
  4.7 0.7 convert.51
  5.4 0.7 convert.52
  6.1 0.7 convert.53
  6.8 0.7 convert.56
  7.5 0.1 fusion.1
  7.6 0.1 stack.68
  7.7 0.6 convert_element_type.4.vectors_in
  8.3 198.5 %layer.1 = (bf16[256,768]{1,0:T(8,128)(2,1)}, f32[256,768]{1,0:T(8,128)}, f32[16,192]{1,0:T(8,128)}, f32[192,2304]{1,0:T(8,128)}, f32[192,768]{1,0:T(8,128)}, /*index=5*/f32[192,3072]{1,0:T(8,128)}, f32[768,768]{1,0:T(8,128)}) custom-call(bf16[256,768]{1,0:T(8,128)(2,1)} %bitcast.13, bf16[256,768]{1,0:T(8,128)(2,1)} %bitcast.14, s32[1]{0:T(128)S(6)} %copy.37.count_in, ...), custom_call_target="tpu_custom_call" | custom-call | tf_op jit(solution)/shard_map/layer/pallas_call | solution.py:908
  206.8 0.0 copy-start.2
  206.8 0.8 slice.54
  207.6 1.6 fusion
  209.2 0.7 reshape.49
  209.9 1.8 copy.38
  211.7 0.0 copy-start.3
  211.7 2.1 copy.39
  213.8 0.0 copy-done.2
  213.8 0.0 copy-start.1
  213.8 1.2 copy.40
  215.0 0.0 copy-done.3
  215.0 0.8 copy.41
  215.8 0.5 copy-done.1
  216.3 0.0 copy-start
  216.3 1.4 copy.42
  217.7 1.1 copy-done
  218.8 1.4 copy.43
  (13 shorter events, 0.1 us)
Async XLA Ops:
  206.8 7.0 %copy-start.2 = (f32[192,2304]{1,0:T(8,128)S(1)}, f32[192,2304]{1,0:T(8,128)}, u32[]{:S(2)}) copy-start(f32[192,2304]{1,0:T(8,128)} %get-tuple-element.60) | copy-start | bytes 5308420
  211.7 3.3 %copy-start.3 = (f32[192,768]{1,0:T(8,128)S(1)}, f32[192,768]{1,0:T(8,128)}, u32[]{:S(2)}) copy-start(f32[192,768]{1,0:T(8,128)} %get-tuple-element.63) | copy-start | bytes 1769476
  213.8 2.5 %copy-start.1 = (f32[192,3072]{1,0:T(8,128)S(1)}, f32[192,3072]{1,0:T(8,128)}, u32[]{:S(2)}) copy-start(f32[192,3072]{1,0:T(8,128)} %get-tuple-element.67) | copy-start | bytes 7077892
  216.3 2.5 %copy-start = (f32[768,768]{1,0:T(8,128)S(1)}, f32[768,768]{1,0:T(8,128)}, u32[]{:S(2)}) copy-start(f32[768,768]{1,0:T(8,128)} %get-tuple-element.69) | copy-start | bytes 7077892

commit v2 on v0

v2 whole, which is shorter than its diff:
```python
import functools
import types

import jax
import jax.numpy as jnp
from jax import lax
from jax.experimental import pallas as pl
from jax.experimental.pallas import tpu as pltpu
from jax.sharding import PartitionSpec as P

D = 768
HD = 64
EPSILON = 1e-06
GROUP = 4
SLICE = D // GROUP
LOCAL_HEADS = SLICE // HD
HALF = D // 2
TILE = 128
PAIR = SLICE // 2
PIECE = SLICE // 4
QKV = 3 * SLICE
BRAIN = jnp.bfloat16
SINGLE = jnp.float32
MESH = pl.DeviceIdType.MESH

G1, B1, BO, G2, B2, C2, BQ, BV, C1 = range(9)
VECTOR_ROWS = 16

WEIGHTS = (
    (GROUP, D, False, ((0, 128, True), (128, 128, True), (256, 128, True), (384, 128, True), (512, 256, False))),
    (GROUP, D, True, ((0, 128, True), (128, 128, True), (256, 128, True), (384, 128, True), (512, 256, False))),
    (1, D, False, ((0, 768, False),)),
    (GROUP, 640, True, ((0, 128, True), (128, 128, True), (256, 128, True), (384, 128, True), (512, 128, True))),
)
DOWN, UP, OUT, QKVS = range(4)
ITEMS = sum(len(parts) for _, _, _, parts in WEIGHTS)

MIXES = (((0, 0), (0, 1)), ((0, 2), (1, 2)), ((1, 0), (1, 1)))


PLAN = (
    (),
    (),
    (1, 41, 11, 21),
    (),
    (91, 31),
    (2, 51),
    (12, 61),
    (),
    (22, 3, 4),
    (32, 13, 14),
    (),
    (52, 23, 24, 71),
    (81, 33, 62),
    (42, 72, 53),
    (5, 34, 82),
    (),
    (15, 92, 63),
    (25,),
    (),
    (73, 35, 43, 44, 111, 83, 101),
    (),
    (74, 121, 84, 131, 93, 141, 75, 64, 54, 112, 151, 85, 122, 45, 65, 113, 132, 102),
    (55, 123, 142, 114, 133, 152),
    (124, 94, 115, 134, 125, 143, 103, 104, 153, 144, 135, 154, 95, 145, 105, 155),
)


class Names:
    def __init__(self):
        self.total = 0

    def take(self, count):
        first = self.total
        self.total += count
        return first


ids = Names()
ID_TOKENS = ids.take(6)
ID_COTANGENT = ids.take(6)
ID_GRADIENT = ids.take(6)
ID_VECTORS = ids.take(3)
ID_QKV = ids.take(9)
ID_OUT = ids.take(9)
ID_UP = ids.take(9)
ID_MIX = ids.take(9)
ID_SUM_TWO = ids.take(6)
ID_SUM_RESULT = ids.take(6)
ID_SUM_ONE = ids.take(6)
ID_SMALL = ids.take(3)
ID_WEIGHTS = ids.take(9 * ITEMS)
COPIES = ids.total
LOCALS = 32


def to_single(value):
    return value.astype(SINGLE)


def rounded(value):
    return value.astype(BRAIN).astype(SINGLE)


def dot(left, right, left_dim, right_dim):
    return lax.dot_general(
        left, right, (((left_dim,), (right_dim,)), ((), ())), preferred_element_type=SINGLE
    )


def normalize(value):
    mean = jnp.sum(value, axis=-1, keepdims=True) * (1.0 / D)
    centred = value - mean
    spread = jnp.sum(centred * centred, axis=-1, keepdims=True) * (1.0 / D)
    scale = lax.rsqrt(spread + EPSILON)
    return centred * scale, scale


def norm_back(grad, normal, scale, gain):
    scaled = grad * gain
    first = jnp.sum(scaled, axis=-1, keepdims=True) * (1.0 / D)
    second = jnp.sum(scaled * normal, axis=-1, keepdims=True) * (1.0 / D)
    return scale * (scaled - first - normal * second)


def row_sum(value):
    return jnp.sum(value, axis=0, keepdims=True)


def gathered(fields, refs):
    result, refs = {}, list(refs)
    for name, count in fields:
        result[name] = [refs.pop(0) for _ in range(count)] if count > 1 else refs.pop(0)
    return types.SimpleNamespace(**result)


def counted(fields):
    return [(name, len(entry) if isinstance(entry, list) else 1) for name, entry in fields.items()]


def flat(fields):
    result = []
    for entry in fields.values():
        result += entry if isinstance(entry, list) else [entry]
    return result


def kernel(replicas, fields, *refs):
    r = gathered(fields, refs)
    levels = (replicas // 8).bit_length() - 1
    slot = r.tokens_in.shape[1]
    pair = 2 * slot
    length = GROUP * slot

    shard = lax.axis_index("shard")
    replica = lax.axis_index("replica")
    chip = shard // 2
    core = shard % 2
    y = replica % 2
    z_low = (replica // 2) % 2
    z_high = (replica // 4) % 2
    inner = (z_low + z_high) % 2 == 1
    edge = (z_low + z_high) % 2 == 0
    block_of_eight = replica // 8
    y_peer = replica + 1 - 2 * y
    z_pair = replica + 2 * (1 - 2 * z_low)

    def mate(step):
        return 2 * ((chip + step // 2) % 2) + (shard + step) % 2

    finals, conditional = [], []

    def remote(source, target, index, **where):
        return pltpu.make_async_remote_copy(
            src_ref=source,
            dst_ref=target,
            send_sem=r.send.at[index],
            recv_sem=r.recv.at[index],
            device_id=where,
            device_id_type=MESH,
        )

    def push(make, *arguments):
        make(*arguments).start()
        finals.append(functools.partial(make, *arguments))

    def push_if(condition, make, *arguments):
        @pl.when(condition)
        def _():
            make(*arguments).start()

        conditional.append((condition, functools.partial(make, *arguments)))

    def local(source, target, index):
        return pltpu.make_async_copy(source, target, r.near.at[index])

    def at(index, size, offset=0):
        return pl.ds(pl.multiple_of(index * size + offset, size), size)

    def here(ref, clip):
        return ref.at[clip, at(shard, slot), :]

    qkv_load = local(r.qkv_in, r.qkv_wide, 0)
    token_loads = [local(r.tokens_in.at[clip], here(r.tokens, clip), 1 + clip) for clip in (0, 1)]
    vector_loads = [
        local(r.vectors_in[row], r.vectors_raw[row], 3 + row)
        for row in range(9)
    ]
    cotangent_loads = [
        local(r.cotangent_in.at[clip], here(r.cotangent, clip), 12 + clip) for clip in (0, 1)
    ]
    wide_loads = [
        local(r.up_in, r.up_wide, 14),
        local(r.out_in, r.out_wide, 15),
        local(r.down_in, r.down_wide, 16),
    ]
    for load in [qkv_load] + token_loads + vector_loads + cotangent_loads + wide_loads:
        load.start()
    barrier = pltpu.get_barrier_semaphore()
    for step in (1, 2, 3):
        pl.semaphore_signal(barrier, inc=1, device_id={"shard": mate(step)}, device_id_type=MESH)

    def greet(step, carry):
        peer = (replica + step) % replicas
        pl.semaphore_signal(barrier, inc=1, device_id={"replica": peer}, device_id_type=MESH)
        return carry

    lax.fori_loop(1, replicas, greet, 0)
    qkv_load.wait()
    for member in range(GROUP):
        left = member * SLICE
        r.qkv_cut[member] = jnp.concatenate(
            [
                r.qkv_wide[:, part * D + left : part * D + left + SLICE].astype(BRAIN)
                for part in range(3)
            ],
            axis=1,
        )
    for load in token_loads + vector_loads:
        load.wait()
    pl.semaphore_wait(barrier, replicas + 2)

    def gather_part(buffer, clip, member):
        return buffer.at[clip, at(member, slot), :]

    def gather_near(buffer, base, clip):
        part = gather_part(buffer, clip, shard)
        return remote(part, part, base + 3 * clip, shard=mate(1))

    def gather_across(buffer, base, clip):
        part = gather_part(buffer, clip, shard)
        return remote(part, part, base + 3 * clip + 1, shard=mate(2))

    def gather_on(buffer, base, clip):
        part = gather_part(buffer, clip, mate(2))
        return remote(part, part, base + 3 * clip + 2, shard=mate(1))

    def gather_start(buffer, base, clip):
        push(gather_across, buffer, base, clip)
        push(gather_near, buffer, base, clip)

    def gather_forward(buffer, base, clip):
        gather_across(buffer, base, clip).wait_recv()
        push(gather_on, buffer, base, clip)

    def quarter(member, y_side, z_side):
        return at((member * 2 + y_side) * 2 + z_side, PIECE)

    def share_across(cut, buffer, base, step):
        source = buffer.at[quarter(shard, y, z_low), :]
        if cut is not None:
            source = cut.at[mate(step), at(2 * y + z_low, PIECE), :]
        return remote(
            source, buffer.at[quarter(shard, y, z_low), :], base + step - 2, shard=mate(step)
        )

    def share_z(buffer, base, step):
        part = buffer.at[quarter(mate(step), y, z_low), :]
        return remote(part, part, base + step, replica=z_pair)

    def share_y(buffer, base, step, second):
        side = 1 - z_low if second else z_low
        part = buffer.at[quarter(mate(step), y, side), :]
        return remote(part, part, base + 2 * second + 2 + step, replica=y_peer)

    def share_near(cut, buffer, base):
        target = buffer.at[at(shard, SLICE), :]
        source = target if cut is None else cut.at[mate(1)]
        return remote(source, target, base + 8, shard=mate(1))

    def share_start(cut, buffer, base, steps):
        for step in steps:
            push(share_across, cut, buffer, base, step)
        push(share_near, cut, buffer, base)

    def share_on(cut, buffer, base, steps):
        for step in steps:
            share_across(cut, buffer, base, step).wait_recv()
            push(share_z, buffer, base, step)
            push(share_y, buffer, base, step, 0)

    def share_last(buffer, base, steps):
        for step in steps:
            share_z(buffer, base, step).wait_recv()
            push(share_y, buffer, base, step, 1)

    def share_wait(cut, buffer, base, steps):
        for step in steps:
            share_y(buffer, base, step, 0).wait_recv()
            share_y(buffer, base, step, 1).wait_recv()
        share_near(cut, buffer, base).wait_recv()

    BOTH, ONE = (2, 3), (2,)

    share_start(r.qkv_cut, r.qkv_own, ID_QKV, BOTH)
    gather_start(r.tokens, ID_TOKENS, 0)
    for row in range(8):
        r.vectors[shard, row : row + 1, :] = rounded(
            r.vectors_raw[row][...].reshape(1, SLICE)
        )
    long_row = rounded(r.vectors_raw[8][...].reshape(1, D))
    for part in range(GROUP):
        r.vectors[shard, C1 + part : C1 + part + 1, :] = long_row[
            :, part * SLICE : (part + 1) * SLICE
        ]
    r.vectors[shard, C1 + GROUP :, :] = jnp.zeros((VECTOR_ROWS - C1 - GROUP, SLICE), SINGLE)

    def send_vectors(step):
        return remote(
            r.vectors.at[shard], r.vectors.at[shard], ID_VECTORS + step - 1, shard=mate(step)
        )

    for step in (1, 2, 3):
        push(send_vectors, step)
    for load in wide_loads:
        load.wait()
    for member in range(GROUP):
        r.up_cut[member] = r.up_wide[:, member * D : (member + 1) * D].astype(BRAIN)
    r.out_all[at(shard, SLICE), :] = r.out_wide[...].astype(BRAIN)
    share_start(None, r.out_all, ID_OUT, ONE)
    share_start(r.up_cut, r.up_own, ID_UP, BOTH)
    gather_start(r.tokens, ID_TOKENS, 1)

    r.qkv_own[at(shard, SLICE), :] = r.qkv_cut[shard]
    share_on(r.qkv_cut, r.qkv_own, ID_QKV, BOTH)
    for load in cotangent_loads:
        load.wait()
    second_live = to_single(jnp.minimum(r.count_in[0] - 1, 1))
    own = at(shard, slot)
    r.cotangent[1, own, :] = (to_single(r.cotangent[1, own, :]) * second_live).astype(BRAIN)
    r.up_own[at(shard, SLICE), :] = r.up_cut[shard]
    r.down_own[...] = r.down_wide[...].astype(BRAIN)
    r.columns[...] = jnp.zeros_like(r.columns)
    share_last(r.qkv_own, ID_QKV, BOTH)
    gather_forward(r.tokens, ID_TOKENS, 0)

    def whole(row):
        return jnp.concatenate([r.vectors[member, row : row + 1, :] for member in range(GROUP)], 1)

    def mine(row):
        return r.vectors[shard, row : row + 1, :]

    for step in (1, 2, 3):
        send_vectors(step).wait_recv()
    share_wait(r.qkv_cut, r.qkv_own, ID_QKV, BOTH)
    scale_row = jnp.where(lax.broadcasted_iota(jnp.int32, (1, QKV), 1) < SLICE, HD**-0.5, 1.0)
    qkv_bias = jnp.concatenate([mine(BQ), jnp.zeros((1, SLICE), SINGLE), mine(BV)], 1)

    def project(clip, side):
        rows = at((chip + side) % 2, pair)
        normal, _ = normalize(to_single(r.tokens[clip, rows, :]))
        hidden = (normal * whole(G1) + whole(B1)).astype(BRAIN)
        r.hidden_one[clip, rows, :] = hidden
        product = (dot(hidden, r.qkv_own[...], 1, 0) + qkv_bias) * scale_row
        r.pairs[clip, rows, :] = product.astype(BRAIN)

    def mix_near(part):
        ref = r.mixed.at[shard, part]
        return remote(ref, ref, ID_MIX + 3 * part, shard=mate(1))

    def mix_across(part):
        ref = r.mixed.at[shard, part]
        return remote(ref, ref, ID_MIX + 3 * part + 1, shard=mate(2))

    def mix_on(part):
        ref = r.mixed.at[mate(2), part]
        return remote(ref, ref, ID_MIX + 3 * part + 2, shard=mate(1))

    def mix_forward(part):
        mix_across(part).wait_recv()
        push(mix_on, part)

    def head_of(ref, clip, left):
        return ref[clip, :, left : left + HD]

    def attend(part, place):
        clip, head = MIXES[part][place]
        query = head_of(r.pairs, clip, head * HD)
        key = head_of(r.pairs, clip, SLICE + head * HD)
        value = head_of(r.pairs, clip, 2 * SLICE + head * HD)
        scores = dot(key, query, 1, 1)
        highest = jnp.max(scores, axis=0, keepdims=True)
        expanded = jnp.exp(scores - highest)
        softened = expanded * (1.0 / row_sum(expanded))
        r.soft[clip * LOCAL_HEADS + head] = softened
        mixture = dot(value.T, softened.astype(BRAIN), 1, 0).T.astype(BRAIN)
        r.mixed[shard, part, :, place * HD : (place + 1) * HD] = mixture

    def mix_start(part):
        push(mix_across, part)
        push(mix_near, part)

    gather_near(r.tokens, ID_TOKENS, 0).wait_recv()
    project(0, 0)
    gather_on(r.tokens, ID_TOKENS, 0).wait_recv()
    project(0, 1)
    attend(0, 0)
    share_on(None, r.out_all, ID_OUT, ONE)
    share_on(r.up_cut, r.up_own, ID_UP, BOTH)
    attend(0, 1)
    mix_start(0)
    attend(1, 0)
    gather_near(r.tokens, ID_TOKENS, 1).wait_recv()
    project(1, 0)
    gather_forward(r.tokens, ID_TOKENS, 1)
    gather_on(r.tokens, ID_TOKENS, 1).wait_recv()
    project(1, 1)
    attend(1, 1)
    mix_start(1)
    gather_start(r.cotangent, ID_COTANGENT, 0)
    share_last(r.out_all, ID_OUT, ONE)
    share_last(r.up_own, ID_UP, BOTH)
    mix_forward(0)
    attend(2, 0)
    attend(2, 1)
    mix_start(2)
    gather_start(r.cotangent, ID_COTANGENT, 1)

    def out_on():
        part = r.out_all.at[at(mate(2), SLICE), :]
        return remote(part, part, ID_OUT + 1, shard=mate(1))

    share_wait(None, r.out_all, ID_OUT, ONE)
    push(out_on)
    mix_forward(1)
    out_on().wait_recv()
    for part in (0, 1):
        mix_near(part).wait_recv()
        mix_on(part).wait_recv()
    share_wait(r.up_cut, r.up_own, ID_UP, BOTH)

    def sum_near(which, base, clip, kind):
        return remote(
            r.sum_sent.at[which, clip, kind],
            r.sum_near.at[which, clip, kind],
            base + 3 * clip + kind,
            shard=mate(1),
        )

    def sum_far(which, base, clip):
        return remote(
            r.sum_sent.at[which, clip, 2],
            r.sum_far.at[which, clip],
            base + 3 * clip + 2,
            shard=mate(2),
        )

    def sum_kept(which, clip, kind):
        if which == 0:
            return r.sum_own.at[clip, kind]
        return r.up_wide.at[0:slot, at(2 * clip + kind, D)]

    def sum_step(which, base, clip, kind, value):
        r.stage[...] = value
        r.sum_sent[which, clip, kind] = r.stage[at(1 - core, slot), :].astype(BRAIN)
        sum_kept(which, clip, kind)[...] = r.stage[at(core, slot), :]
        remote(
            r.sum_sent.at[which, clip, kind],
            r.sum_near.at[which, clip, kind],
            base + 3 * clip + kind,
            shard=mate(1),
        ).start()

    def sum_on(which, base, clip):
        sum_near(which, base, clip, 0).wait_recv()
        r.sum_sent[which, clip, 2] = (
            sum_kept(which, clip, 0)[...] + to_single(r.sum_near[which, clip, 0])
        ).astype(BRAIN)
        sum_far(which, base, clip).start()

    def sum_end(which, base, clip):
        sum_near(which, base, clip, 0).wait_send()
        sum_near(which, base, clip, 1).wait()
        sum_far(which, base, clip).wait()
        return (
            sum_kept(which, clip, 1)[...]
            + to_single(r.sum_near[which, clip, 1])
            + to_single(r.sum_far[which, clip])
        )

    def rows_of(kind):
        return at((chip + 1 + kind) % 2, pair)

    long_bias = jnp.concatenate(
        [r.vectors[shard, C1 + part : C1 + part + 1, :] for part in range(GROUP)], 1
    )

    def pass_on(across, on):
        across.wait_recv()
        on.start()

    def feed(clip, kind, carry):
        rows = rows_of(kind)
        if clip == 0:

            @pl.when(kind == 1)
            def _():
                pass_on(
                    gather_across(r.cotangent, ID_COTANGENT, 0),
                    gather_on(r.cotangent, ID_COTANGENT, 0),
                )

        total = to_single(r.tokens[clip, rows, :]) + whole(BO)
        for member in range(GROUP):
            heads = jnp.concatenate(
                [
                    r.mixed[member, 2 * clip, rows, :],
                    r.mixed[member, 1, rows, clip * HD : (clip + 1) * HD],
                ],
                1,
            )
            total += dot(heads, r.out_all[member * SLICE : (member + 1) * SLICE, :], 1, 0)

        @pl.when(kind == 1)
        def _():
            r.stage[...] = total
            r.middle_own[clip] = r.stage[at(core, slot), :]

        normal, _ = normalize(total)
        hidden = (normal * whole(G2) + whole(B2)).astype(BRAIN)
        r.hidden_two[clip, rows, :] = hidden
        lifted = dot(hidden, r.up_own[...], 1, 0) + long_bias
        share = 0.5 + 0.5 * lax.erf(lifted * (0.5**0.5))
        r.active[clip, rows, :] = (lifted * share).astype(BRAIN)
        r.down_wide[at(kind, pair), :] = share + lifted * jnp.exp(lifted * lifted * -0.5) * 0.3989422804014327
        return carry

    def feed_back(clip, kind, carry):
        rows = rows_of(kind)
        if clip == 0:

            @pl.when(kind == 1)
            def _():
                pass_on(mix_across(2), mix_on(2))

        down = r.cotangent[clip, rows, :]
        r.columns[0:1, :] += row_sum(to_single(down))
        grad = (dot(down, r.down_own[...], 1, 1) * r.down_wide[at(kind, pair), :]).astype(BRAIN)
        r.lifted_grad[clip, rows, :] = grad
        r.columns[1:2, :] += row_sum(to_single(grad))
        sum_step(0, ID_SUM_TWO, clip, kind, dot(grad, r.up_own[...], 1, 1))
        return carry

    def both(step, clip):
        lax.fori_loop(0, 2, functools.partial(step, clip), 0)

    both(feed, 0)
    finals.append(functools.partial(gather_on, r.cotangent, ID_COTANGENT, 0))
    gather_near(r.cotangent, ID_COTANGENT, 0).wait_recv()
    gather_on(r.cotangent, ID_COTANGENT, 0).wait_recv()
    both(feed_back, 0)
    finals.append(functools.partial(mix_on, 2))
    mix_near(2).wait_recv()
    mix_on(2).wait_recv()
    sum_on(0, ID_SUM_TWO, 0)
    both(feed, 1)
    gather_forward(r.cotangent, ID_COTANGENT, 1)
    gather_near(r.cotangent, ID_COTANGENT, 1).wait_recv()
    gather_on(r.cotangent, ID_COTANGENT, 1).wait_recv()
    stages = []

    def weight(index, number, crosses, columns, y_first, grad):
        base = ID_WEIGHTS + 9 * number
        halves, line, middle, full = (
            refs[index] for refs in (r.halves, r.lines, r.middles, r.fulls)
        )
        crossed = r.crossed[index // 2] if crosses else None
        blocks = grad.shape[0]
        cols = slice(columns[0], columns[0] + columns[1])
        size = PAIR if y_first else PIECE
        first, first_peer, second, second_peer = (
            (y, y_peer, z_low, z_pair) if y_first else (z_low, z_pair, y, y_peer)
        )
        source = (crossed if crosses else line).at[:, 0:size, cols]
        held = slice(0, PAIR) if y_first else at(second, PIECE)

        def final_rows(side):
            return at(first, PAIR) if y_first else at(2 * first + side, PIECE)

        def first_copy():
            return remote(
                grad.at[:, at(1 - first, PAIR), cols],
                halves.at[:, :, cols],
                base,
                replica=first_peer,
            )

        def second_copy():
            given = slice(0, PAIR) if y_first else at(1 - second, PIECE)
            return remote(
                halves.at[:, given, cols],
                line.at[:, 0:size, cols],
                base + 1,
                replica=second_peer,
            )

        def far_copy():
            apart = 2 if y_first else 4
            return remote(
                halves.at[:, held, cols],
                middle.at[:, 0:size, cols],
                base + 2,
                replica=replica + apart * (1 - 2 * z_high),
            )

        def farther_copy(level):
            apart = 8 * 2**level * (1 - 2 * ((block_of_eight // 2**level) % 2))
            return pltpu.make_async_remote_copy(
                src_ref=line.at[:, 0:size, cols],
                dst_ref=r.extras[index].at[level, :, 0:size, cols],
                send_sem=r.send_all.at[number + 1, level],
                recv_sem=r.recv_all.at[number + 1, level],
                device_id={"replica": replica + apart},
                device_id_type=MESH,
            )

        def cross_copy(step):
            return remote(
                line.at[mate(step), 0:size, cols],
                crossed.at[shard, 0:size, cols],
                base + 2 + step,
                shard=mate(step),
            )

        def second_back():
            return remote(
                source, full.at[:, final_rows(second), cols], base + 6, replica=second_peer
            )

        def first_back(late):
            if not late:
                return remote(
                    source, full.at[:, final_rows(second), cols], base + 7, replica=first_peer
                )
            ref = full.at[:, final_rows(1 - second), cols]
            return remote(ref, ref, base + 8 - y_first, replica=first_peer)

        def start():
            push(first_copy)

        def second_start():
            first_copy().wait_recv()
            for block in range(blocks):
                halves[block, :, cols] = (
                    to_single(grad[block, at(first, PAIR), cols])
                    + to_single(halves[block, :, cols])
                ).astype(BRAIN)
            if y_first:
                push_if(edge, second_copy)
            else:
                push(second_copy)

        def far_start():
            second_copy().wait_recv()
            for block in range(blocks):
                halves[block, held, cols] = (
                    to_single(halves[block, held, cols]) + to_single(line[block, 0:size, cols])
                ).astype(BRAIN)
            far_copy().start()

        def cross_start():
            far_copy().wait()
            for block in range(blocks):
                line[block, 0:size, cols] = (
                    to_single(halves[block, held, cols]) + to_single(middle[block, 0:size, cols])
                ).astype(BRAIN)
            for level in range(levels):
                farther_copy(level).start()
                farther_copy(level).wait()
                line[:, 0:size, cols] = (
                    to_single(line[:, 0:size, cols])
                    + to_single(r.extras[index][level, :, 0:size, cols])
                ).astype(BRAIN)
            if crosses:
                crossed[shard, 0:size, cols] = line[shard, 0:size, cols]
                for step in (2, 3, 1):
                    cross_copy(step).start()

        def back_start():
            if crosses:
                for step in (1, 2, 3):
                    cross_copy(step).wait()
            second_back().start()
            first_back(False).start()
            for block in range(blocks):
                full[block, final_rows(second), cols] = source[block]
            conditional.append((inner if y_first else None, second_back))
            conditional.append(
                (inner if y_first else None, functools.partial(first_back, False))
            )

        def back_on():
            second_back().wait_recv()
            push(first_back, True)

        def back_end():
            if not y_first:
                first_back(False).wait_recv()
            first_back(True).wait_recv()

        def only(condition, step):
            def run_if():
                pl.when(condition)(step)

            return run_if if y_first else step

        def edge_on():
            @pl.when(edge)
            def _():
                second_back().wait_recv()

            push_if(edge, first_back, True)

        stages.append(
            (
                start,
                second_start,
                only(inner, far_start),
                only(inner, cross_start),
                only(inner, back_start),
                edge_on if y_first else back_on,
                back_end,
            )
        )

    grads = (r.up_cut, r.up_grad, r.out_grad, r.qkv_grad)
    for index, (_, _, crosses, parts) in enumerate(WEIGHTS):
        for start_column, width, y_first in parts:
            weight(index, len(stages), crosses, (start_column, width), y_first, grads[index])

    def run(*codes):
        for code in codes:
            stages[code // 10][code % 10]()

    rest = []
    for item in finals:
        if item.func in (share_across, share_near) and item.args[0] is r.up_cut:
            item().wait_send()
        else:
            rest.append(item)
    finals[:] = rest

    def cut_product(target, left, right, width):
        for part in range(2):
            product = dot(
                left[:, :, part * HALF : (part + 1) * HALF].reshape(2 * length, HALF),
                right[...].reshape(2 * length, width),
                0,
                0,
            )
            for half in range(2):
                target[2 * part + half, :, 0:width] = product[
                    half * SLICE : (half + 1) * SLICE
                ].astype(BRAIN)

    steps = iter(PLAN)

    def plan():
        run(*next(steps))

    cut_product(r.up_cut, r.active, r.cotangent, D)
    run(40, 0, 10, 20, 30)
    plan()
    both(feed_back, 1)
    sum_on(0, ID_SUM_TWO, 1)
    cut_product(r.up_grad, r.hidden_two, r.lifted_grad, D)
    run(90, 50, 60, 70, 80)
    plan()

    for clip in (0, 1):
        grad_two = sum_end(0, ID_SUM_TWO, clip)
        normal, scale = normalize(r.middle_own[clip])
        r.columns[2:3, :] += row_sum(grad_two * normal)
        r.columns[3:4, :] += row_sum(grad_two)
        total = to_single(r.cotangent[clip, own, :]) + norm_back(
            grad_two, normal, scale, whole(G2)
        )
        r.down_wide[4 * slot + clip * slot : 5 * slot + clip * slot, :] = total
        r.gradient[clip, own, :] = total.astype(BRAIN)
        gather_start(r.gradient, ID_GRADIENT, clip)
        plan()

    def lower(clip, kind, carry):
        value = dot(r.active[clip, rows_of(kind), :], r.down_own[...], 1, 0)
        sum_step(1, ID_SUM_RESULT, clip, kind, value)
        return carry

    for clip in (0, 1):
        both(lower, clip)
        plan()

    def back_out(clip):
        gather_near(r.gradient, ID_GRADIENT, clip).wait_recv()
        gather_on(r.gradient, ID_GRADIENT, clip).wait_recv()
        grad = r.gradient[clip]
        r.columns[4:5, :] += row_sum(to_single(grad))
        r.mixed_grad[clip] = dot(grad, r.out_all[at(shard, SLICE), :], 1, 1).astype(BRAIN)

    def attend_back(clip, head):
        query = head_of(r.pairs, clip, head * HD)
        key = head_of(r.pairs, clip, SLICE + head * HD)
        value = head_of(r.pairs, clip, 2 * SLICE + head * HD)
        grad = head_of(r.mixed_grad, clip, head * HD)
        softened = r.soft[clip * LOCAL_HEADS + head]
        grad_soft = dot(value, grad, 1, 1)
        inner = row_sum(grad_soft * softened)
        grad_scores = (softened * (grad_soft - inner)).astype(BRAIN)
        entries = (
            (dot(key.T, grad_scores, 1, 0).T * HD**-0.5).astype(BRAIN),
            dot(grad_scores, query, 1, 0).astype(BRAIN),
            dot(softened.astype(BRAIN), grad, 1, 0).astype(BRAIN),
        )
        for part, entry in enumerate(entries):
            left = part * SLICE + head * HD
            r.pairs_grad[clip, :, left : left + HD] = entry

    for clip in (0, 1):
        gather_forward(r.gradient, ID_GRADIENT, clip)
        plan()
        back_out(clip)
        plan()
        if clip == 1:
            for other in (0, 1):
                sum_on(1, ID_SUM_RESULT, other)
        for head in range(LOCAL_HEADS):
            attend_back(clip, head)
            plan()
    product = None
    for clip in (0, 1):
        heads = jnp.concatenate(
            [r.mixed[shard, 2 * clip], r.mixed[shard, 1, :, clip * HD : (clip + 1) * HD]], 1
        )
        term = dot(heads, r.gradient[clip], 0, 0)
        product = term if product is None else product + term
    r.out_grad[0] = product.astype(BRAIN)
    run(100)
    plan()
    cut_product(r.qkv_grad, r.hidden_one, r.pairs_grad, QKV)
    r.qkv_grad[:, :, QKV:] = jnp.zeros((GROUP, SLICE, HD), BRAIN)
    run(110, 120, 130, 140, 150)
    plan()

    def back_project(clip, kind, carry):
        grad = r.pairs_grad[clip, rows_of(kind), :]
        r.columns[5:6, 0:QKV] += row_sum(to_single(grad))
        sum_step(0, ID_SUM_ONE, clip, kind, dot(grad, r.qkv_own[...], 1, 1))
        return carry

    for clip in (0, 1):
        both(back_project, clip)
        plan()
    for clip in (0, 1):
        sum_on(0, ID_SUM_ONE, clip)
    plan()
    for clip in (0, 1):
        live = 1.0 if clip == 0 else second_live
        result = r.middle_own[clip] + sum_end(1, ID_SUM_RESULT, clip) + whole(C2)
        r.hidden_one[clip, 0:slot, :] = (result * live).astype(BRAIN)
    result_copy = local(r.hidden_one.at[:, 0:slot, :], r.result_out, 17)
    result_copy.start()
    plan()
    for clip in (0, 1):
        grad_one = sum_end(0, ID_SUM_ONE, clip)
        normal, scale = normalize(to_single(r.tokens[clip, own, :]))
        r.columns[6:7, :] += row_sum(grad_one * normal)
        r.columns[7:8, :] += row_sum(grad_one)
        r.down_wide[4 * slot + clip * slot : 5 * slot + clip * slot, :] += norm_back(grad_one, normal, scale, whole(G1))
    grad_copies = [
        local(
            r.down_wide.at[4 * slot + clip * slot : 5 * slot + clip * slot],
            r.input_grad_out.at[clip],
            18 + 6 * clip,
        )
        for clip in (0, 1)
    ]
    for item in grad_copies:
        item.start()

    for member in range(GROUP):
        cols = slice(member * SLICE, (member + 1) * SLICE)
        for place, row in enumerate((6, 7, 2, 3, 4, 0)):
            r.small_sent[member, place : place + 1, :] = r.columns[row : row + 1, cols]

    def small_copy(step):
        return remote(
            r.small_sent.at[mate(step)],
            r.small_near.at[step - 1],
            ID_SMALL + step - 1,
            shard=mate(step),
        )

    for step in (1, 2, 3):
        push(small_copy, step)
    plan()
    for step in (1, 2, 3):
        small_copy(step).wait_recv()
    summed = r.small_sent[shard, 0:4, :]
    for step in (1, 2, 3):
        summed += r.small_near[step - 1, 0:4, :]
    r.small_all[replica, G1 : G1 + 2, :] = summed[0:2]
    r.small_all[replica, G2 : G2 + 2, :] = summed[2:4]
    r.small_all[replica, BO : BO + 1, :] = r.small_sent[shard, 4:5, :]
    r.small_all[replica, C2 : C2 + 1, :] = r.small_sent[shard, 5:6, :]
    r.small_all[replica, BQ : BQ + 1, :] = r.columns[5:6, 0:SLICE]
    r.small_all[replica, BV : BV + 1, :] = r.columns[5:6, 2 * SLICE : QKV]
    for part in range(GROUP):
        r.small_all[replica, C1 + part : C1 + part + 1, :] = r.columns[
            1:2, part * SLICE : (part + 1) * SLICE
        ]
    r.small_all[replica, C1 + GROUP :, :] = jnp.zeros((VECTOR_ROWS - C1 - GROUP, SLICE), SINGLE)

    def spread_copy(step):
        return pltpu.make_async_remote_copy(
            src_ref=r.small_all.at[replica],
            dst_ref=r.small_all.at[replica],
            send_sem=r.send_all.at[0, step],
            recv_sem=r.recv_all.at[0, step],
            device_id={"replica": (replica + step) % replicas},
            device_id_type=MESH,
        )

    def spread_start(step, carry):
        spread_copy(step).start()
        return carry

    lax.fori_loop(1, replicas, spread_start, 0)
    plan()

    def spread_wait(step, carry):
        spread_copy(step).wait()
        return carry

    lax.fori_loop(1, replicas, spread_wait, 0)
    small_sum = r.small_all[0]
    for step in range(1, replicas):
        small_sum += r.small_all[step]
    r.small_all[0] = small_sum
    copies = grad_copies + [result_copy, local(r.small_all.at[0], r.small_out, 19)]
    copies[-1].start()
    run(106)
    copies.append(local(r.fulls[OUT], r.sums_out[OUT], 20))
    copies[-1].start()
    run(6, 16, 26, 36, 46)
    copies.append(local(r.fulls[DOWN], r.sums_out[DOWN], 21))
    copies[-1].start()
    run(116, 126, 136, 146, 156)
    copies.append(local(r.fulls[QKVS], r.sums_out[QKVS], 22))
    copies[-1].start()
    run(56, 66, 76, 86, 96)
    copies.append(local(r.fulls[UP], r.sums_out[UP], 23))
    copies[-1].start()
    for item in finals:
        item().wait_send()
    for condition, item in conditional:
        if condition is None:
            item().wait_send()
        else:

            @pl.when(condition)
            def _():
                item().wait_send()

    for item in copies:
        item.wait()


def finish(fields, *refs):
    r = gathered(fields, refs)
    units = []

    def unit(source, held, wide, target, widen):
        index = len(units)
        units.append(
            (
                pltpu.make_async_copy(source, held, r.near.at[index]),
                pltpu.make_async_copy(wide, target, r.near.at[index]),
                widen,
            )
        )

    def keep():
        pass

    def down(index):
        rows = slice(index * SLICE, (index + 1) * SLICE)

        def widen():
            r.wide[DOWN][rows, :] = to_single(r.narrow[DOWN][index])

        unit(
            r.sums_in[DOWN].at[index],
            r.narrow[DOWN].at[index],
            r.wide[DOWN].at[rows],
            r.results[DOWN].at[rows],
            widen,
        )

    def up(index):
        cols = slice(index * D, (index + 1) * D)

        def widen():
            r.wide[UP][:, cols] = to_single(r.narrow[UP][index])

        unit(
            r.sums_in[UP].at[index],
            r.narrow[UP].at[index],
            r.wide[UP].at[:, cols],
            r.results[UP].at[:, cols],
            widen,
        )

    def qkv(index):
        rows = slice(index * PIECE, (index + 1) * PIECE)

        def widen():
            for part in range(3):
                cols = slice(part * SLICE, (part + 1) * SLICE)
                r.wide[QKVS][rows, part * D : (part + 1) * D] = to_single(
                    jnp.concatenate(
                        [r.narrow[QKVS][member, rows, cols] for member in range(GROUP)], 1
                    )
                )

        unit(
            r.sums_in[QKVS].at[:, rows],
            r.narrow[QKVS].at[:, rows],
            r.wide[QKVS].at[rows],
            r.results[QKVS].at[rows],
            widen,
        )

    def out():
        def widen():
            r.wide[OUT][...] = to_single(r.narrow[OUT][0])

        unit(r.sums_in[OUT], r.narrow[OUT], r.wide[OUT], r.results[OUT], widen)

    unit(r.input_grad_in, r.input_grad_held, r.input_grad_held, r.input_grad, keep)
    unit(r.result_in, r.result_held, r.result_held, r.result, keep)
    for index in range(GROUP):
        down(index)
        up(index)
    out()
    for index in range(GROUP):
        qkv(index)
    for load, _, _ in units:
        load.start()
    for row in range(8):
        r.vectors[row][...] = r.small_in[row : row + 1, :].reshape(SLICE)
    r.vectors[8][...] = jnp.concatenate(
        [r.small_in[C1 + part : C1 + part + 1, :] for part in range(GROUP)], 1
    ).reshape(D)
    for load, store, widen in units:
        load.wait()
        widen()
        store.start()
    for _, store, _ in units:
        store.wait()


def layer(replicas, *arguments):
    (
        tokens, cotangent, clip_count, ln1_gain, ln1_bias, qkv_weight, q_bias, v_bias,
        out_weight, out_bias, ln2_gain, ln2_bias, fc1_weight, fc1_bias, fc2_weight, fc2_bias,
    ) = arguments
    slots, slot, _ = tokens.shape
    length = slot * GROUP
    levels = (replicas // 8).bit_length() - 1
    vectors = (
        ln1_gain, ln1_bias, out_bias, ln2_gain, ln2_bias, fc2_bias, q_bias, v_bias, fc1_bias,
    )
    anywhere = pl.BlockSpec(memory_space=pl.ANY)
    in_memory = pl.BlockSpec(memory_space=pltpu.VMEM)
    in_hbm = pl.BlockSpec(memory_space=pltpu.HBM)
    shape = jax.ShapeDtypeStruct

    inputs = dict(
        tokens_in=anywhere,
        cotangent_in=anywhere,
        count_in=pl.BlockSpec(memory_space=pltpu.SMEM),
        vectors_in=[anywhere] * 9,
        qkv_in=anywhere,
        out_in=anywhere,
        up_in=anywhere,
        down_in=anywhere,
    )
    outputs = dict(
        result_out=shape(tokens.shape, BRAIN),
        input_grad_out=shape(tokens.shape, SINGLE),
        small_out=shape((VECTOR_ROWS, SLICE), SINGLE),
        sums_out=[shape((blocks, SLICE, columns), BRAIN) for blocks, columns, _, _ in WEIGHTS],
    )
    scratch = dict(
        qkv_wide=pltpu.VMEM(qkv_weight.shape, SINGLE),
        out_wide=pltpu.VMEM(out_weight.shape, SINGLE),
        up_wide=pltpu.VMEM(fc1_weight.shape, SINGLE),
        down_wide=pltpu.VMEM(fc2_weight.shape, SINGLE),
        qkv_cut=pltpu.VMEM((GROUP, SLICE, QKV), BRAIN),
        up_cut=pltpu.VMEM((GROUP, SLICE, D), BRAIN),
        qkv_own=pltpu.VMEM((D, QKV), BRAIN),
        up_own=pltpu.VMEM((D, D), BRAIN),
        out_all=pltpu.VMEM((D, D), BRAIN),
        down_own=pltpu.VMEM((D, D), BRAIN),
        vectors=pltpu.VMEM((GROUP, VECTOR_ROWS, SLICE), SINGLE),
        vectors_raw=[pltpu.VMEM(vector.shape, SINGLE) for vector in vectors],
        tokens=pltpu.VMEM((2, length, D), BRAIN),
        cotangent=pltpu.VMEM((2, length, D), BRAIN),
        hidden_one=pltpu.VMEM((2, length, D), BRAIN),
        pairs=pltpu.VMEM((2, length, QKV), BRAIN),
        soft=pltpu.VMEM((2 * LOCAL_HEADS, length, length), SINGLE),
        mixed=pltpu.VMEM((GROUP, 3, length, TILE), BRAIN),
        middle_own=pltpu.VMEM((2, slot, D), SINGLE),
        hidden_two=pltpu.VMEM((2, length, D), BRAIN),
        active=pltpu.VMEM((2, length, D), BRAIN),
        lifted_grad=pltpu.VMEM((2, length, D), BRAIN),
        gradient=pltpu.VMEM((2, length, D), BRAIN),
        mixed_grad=pltpu.VMEM((2, length, SLICE), BRAIN),
        pairs_grad=pltpu.VMEM((2, length, QKV), BRAIN),
        stage=pltpu.VMEM((2 * slot, D), SINGLE),
        sum_sent=pltpu.VMEM((2, 2, 3, slot, D), BRAIN),
        sum_near=pltpu.VMEM((2, 2, 2, slot, D), BRAIN),
        sum_far=pltpu.VMEM((2, 2, slot, D), BRAIN),
        sum_own=pltpu.VMEM((2, 2, slot, D), SINGLE),
        up_grad=pltpu.VMEM((GROUP, SLICE, D), BRAIN),
        out_grad=pltpu.VMEM((1, SLICE, D), BRAIN),
        qkv_grad=pltpu.VMEM((GROUP, SLICE, QKV + HD), BRAIN),
        columns=pltpu.VMEM((8, D), SINGLE),
        small_sent=pltpu.VMEM((GROUP, 8, SLICE), SINGLE),
        small_near=pltpu.VMEM((GROUP - 1, 8, SLICE), SINGLE),
        small_all=pltpu.VMEM((replicas, VECTOR_ROWS, SLICE), SINGLE),
        halves=[pltpu.VMEM((w[0], PAIR, w[1]), BRAIN) for w in WEIGHTS],
        lines=[pltpu.VMEM((w[0], PAIR, w[1]), BRAIN) for w in WEIGHTS],
        middles=[pltpu.VMEM((w[0], PAIR, w[1]), BRAIN) for w in WEIGHTS],
        fulls=[pltpu.VMEM((w[0], SLICE, w[1]), BRAIN) for w in WEIGHTS],
        crossed=[pltpu.VMEM((GROUP, PAIR, w[1]), BRAIN) for w in WEIGHTS if w[2]],
        extras=[
            pltpu.VMEM((levels, w[0], PAIR, w[1]) if levels else (1, 1, 16, TILE), BRAIN)
            for w in WEIGHTS
        ],
        send=pltpu.SemaphoreType.DMA((COPIES,)),
        recv=pltpu.SemaphoreType.DMA((COPIES,)),
        send_all=pltpu.SemaphoreType.DMA((1 + ITEMS, replicas)),
        recv_all=pltpu.SemaphoreType.DMA((1 + ITEMS, replicas)),
        near=pltpu.SemaphoreType.DMA((LOCALS,)),
    )
    sums = pl.pallas_call(
        functools.partial(kernel, replicas, counted(inputs) + counted(outputs) + counted(scratch)),
        out_shape=tuple(flat(outputs)),
        in_specs=flat(inputs),
        out_specs=(anywhere,) * len(flat(outputs)),
        scratch_shapes=flat(scratch),
        compiler_params=pltpu.CompilerParams(
            collective_id=0, has_side_effects=True, vmem_limit_bytes=65000 * 1024
        ),
        name="layer",
    )(
        tokens, cotangent, clip_count, *vectors, qkv_weight, out_weight, fc1_weight, fc2_weight
    )

    matrices = [fc2_weight, fc1_weight, out_weight, qkv_weight]
    last_inputs = dict(
        result_in=in_hbm, input_grad_in=in_hbm, small_in=in_memory, sums_in=[in_hbm] * 4
    )
    last_outputs = dict(
        result=shape(tokens.shape, BRAIN),
        input_grad=shape(tokens.shape, SINGLE),
        results=[shape(array.shape, SINGLE) for array in matrices],
        vectors=[shape(vector.shape, SINGLE) for vector in vectors],
    )
    last_scratch = dict(
        narrow=[pltpu.VMEM((blocks, SLICE, columns), BRAIN) for blocks, columns, _, _ in WEIGHTS],
        wide=[pltpu.VMEM(array.shape, SINGLE) for array in matrices],
        input_grad_held=pltpu.VMEM(tokens.shape, SINGLE),
        result_held=pltpu.VMEM(tokens.shape, BRAIN),
        near=pltpu.SemaphoreType.DMA((16,)),
    )
    values = pl.pallas_call(
        functools.partial(
            finish, counted(last_inputs) + counted(last_outputs) + counted(last_scratch)
        ),
        out_shape=tuple(flat(last_outputs)),
        in_specs=flat(last_inputs),
        out_specs=(anywhere,) * 6 + (in_memory,) * 9,
        scratch_shapes=flat(last_scratch),
        compiler_params=pltpu.CompilerParams(vmem_limit_bytes=60 << 20),
        name="finish",
    )(*sums)
    o = gathered(counted(last_outputs), values)
    return (
        o.result,
        o.input_grad,
        o.vectors[G1],
        o.vectors[B1],
        o.results[QKVS],
        o.vectors[BQ],
        o.vectors[BV],
        o.results[OUT],
        o.vectors[BO],
        o.vectors[G2],
        o.vectors[B2],
        o.results[UP],
        o.vectors[C1],
        o.results[DOWN],
        o.vectors[C2],
    )


def solution(mesh):
    token, vector, matrix = P("replica", "shard", None), P("shard"), P("shard", None)
    return jax.shard_map(
        functools.partial(layer, mesh.shape["replica"]),
        mesh=mesh,
        in_specs=(
            token, token, P("replica"), vector, vector, matrix, vector, vector,
            matrix, vector, vector, vector, matrix, vector, matrix, vector,
        ),
        out_specs=(
            token, token, vector, vector, matrix, vector, vector, matrix,
            vector, vector, vector, matrix, vector, matrix, vector,
        ),
        check_vma=False,
    )
```

time: 737 us -> 137 us (0.19); the launches traced: 728 us -> 137 us
  blocking collectives: 309 us -> 0 us
  waiting for transfers between devices: 244 us -> 0 us
  Pallas kernels: 0 us -> 135 us
  matrix products: 74.1 us -> 0 us
  other arithmetic: 44.7 us -> 0 us
  local copies, waits for them, and re-layouts: 37.9 us -> 0 us
  between operations: 18.4 us -> 1.49 us
    psum x1 -> x0, blocking collectives: 279 us -> none  [local(): lax.psum((sum_gain_one, sum_shift_one, sum_qkv, sum_bias_query, sum_bias_...]
    reduce_scatter x5 -> x0, waiting for transfers between devices: 142 us -> none  [the longest x1 50.6 us: local(): lax.psum_scatter(grad_down.astype(jnp.bfloat16), 'shard', scatter_dimensi...]
    pallas_call x0 -> x2, Pallas kernels: none -> 135 us  [the longest x1 130 us: layer(): pl.pallas_call(functools.partial(kernel, replicas, counted(inputs) + coun...]
    all_gather x5 -> x0, waiting for transfers between devices: 101 us -> none  [the longest x1 34.5 us: local(): lax.all_gather(fc1_weight.astype(brain), 'shard', axis=0, tiled=True)]
    dot_general x24 -> x0, matrix products: 74.1 us -> none  [the longest x4 19.1 us: multiply_by_transpose(): lax.dot_general(left, right, (((1,), (1,)), ((), ())), preferred_element_...]
    convert_element_type x38 -> x0, other arithmetic: 31.1 us -> none  [the longest x5 6.57 us: local(): sum_gain_one, sum_shift_one, sum_qkv, sum_bias_query, sum_bias_value, sum...]
    unnamed x2 -> x0, blocking collectives: 24.6 us -> none
    unnamed x214 -> x0, local copies, waits for them, and re-layouts: 14.9 us -> none
  transfers between devices with their start and end apart: 10 -> 0, of which waited for: 10 -> 0; matrix products, arithmetic and copies ran while one was open for 12% -> 0% of each run, Pallas kernels for 0% -> 0%
where the time goes in v2:
time: 137 us
  Pallas kernels  135 us (99%)
  between operations  1.49 us (1%)
    pallas_call x1, Pallas kernels, layer(): pl.pallas_call(functools.partial(kernel, replicas, counted(inputs) + coun...  130 us
    pallas_call x1, Pallas kernels, layer(): pl.pallas_call(functools.partial(finish, counted(last_inputs) + counted(l...  5.86 us

profile of v2, /device:TPU:0, one launch (start us, length us, event | category | flops | bytes accessed | tf_op | source)
XLA Modules:
  0.0 136.9 jit_solution(14562413440632616056)
XLA Ops:
  1.3 129.5 %layer.1 = (bf16[2,128,768]{2,1,0:T(8,128)(2,1)}, f32[2,128,768]{2,1,0:T(8,128)}, f32[16,192]{1,0:T(8,128)}, bf16[4,192,768]{2,1,0:T(8,128)(2,1)}, bf16[4,192,76...) custom-call(bf16[2,128,768]{2,1,0:T(8,128)(2,1)} %refs_0_.1, ...), custom_call_target="tpu_custom_call" | custom-call | tf_op jit(solution)/shard_map/layer/pallas_call | solution.py:1166
  130.8 5.9 %finish.1 = (bf16[2,128,768]{2,1,0:T(8,128)(2,1)}, f32[2,128,768]{2,1,0:T(8,128)}, f32[768,768]{1,0:T(8,128)}, f32[192,3072]{1,0:T(8,128)}, f32[192,768]{1,0:T(8...) custom-call(bf16[2,128,768]{2,1,0:T(8,128)(2,1)} %get-tuple-element., ...), custom_call_target="tpu_custom_call" | custom-call | tf_op jit(solution)/shard_map/finish/pallas_call | solution.py:1197

commit v3 on v2

--- a/solution.py
+++ b/solution.py
@@ -78,7 +78,7 @@
 
 ids = Names()
 ID_TOKENS = ids.take(6)
-ID_COTANGENT = ids.take(6)
+ID_COTANGENT = ids.take(12)
 ID_GRADIENT = ids.take(6)
 ID_VECTORS = ids.take(3)
 ID_QKV = ids.take(9)
@@ -200,7 +200,13 @@
     def here(ref, clip):
         return ref.at[clip, at(shard, slot), :]
 
-    qkv_load = local(r.qkv_in, r.qkv_wide, 0)
+    def quarter_rows(step):
+        return at((2 * y + z_low + step) % 4, PIECE)
+
+    qkv_loads = [
+        local(r.qkv_in.at[quarter_rows(step)], r.qkv_wide.at[quarter_rows(step)], 25 + step)
+        for step in range(4)
+    ]
     token_loads = [local(r.tokens_in.at[clip], here(r.tokens, clip), 1 + clip) for clip in (0, 1)]
     vector_loads = [
         local(r.vectors_in[row], r.vectors_raw[row], 3 + row)
@@ -214,7 +220,7 @@
         local(r.out_in, r.out_wide, 15),
         local(r.down_in, r.down_wide, 16),
     ]
-    for load in [qkv_load] + token_loads + vector_loads + cotangent_loads + wide_loads:
+    for load in qkv_loads + token_loads + vector_loads + cotangent_loads + wide_loads:
         load.start()
     barrier = pltpu.get_barrier_semaphore()
     for step in (1, 2, 3):
@@ -226,21 +232,28 @@
         return carry
 
     lax.fori_loop(1, replicas, greet, 0)
-    qkv_load.wait()
-    for member in range(GROUP):
-        left = member * SLICE
-        r.qkv_cut[member] = jnp.concatenate(
-            [
-                r.qkv_wide[:, part * D + left : part * D + left + SLICE].astype(BRAIN)
-                for part in range(3)
-            ],
-            axis=1,
-        )
+
+    def cut_rows(step):
+        qkv_loads[step].wait()
+        rows = quarter_rows(step)
+        for member in range(GROUP):
+            left = member * SLICE
+            r.qkv_cut[member, rows, :] = jnp.concatenate(
+                [
+                    r.qkv_wide[rows, part * D + left : part * D + left + SLICE].astype(BRAIN)
+                    for part in range(3)
+                ],
+                axis=1,
+            )
+
+    cut_rows(0)
     for load in token_loads + vector_loads:
         load.wait()
     pl.semaphore_wait(barrier, replicas + 2)
 
     def gather_part(buffer, clip, member):
+        if clip >= 2:
+            return buffer.at[0, at(2 * member + clip - 2, slot // 2), :]
         return buffer.at[clip, at(member, slot), :]
 
     def gather_near(buffer, base, clip):
@@ -288,9 +301,12 @@
         source = target if cut is None else cut.at[mate(1)]
         return remote(source, target, base + 8, shard=mate(1))
 
-    def share_start(cut, buffer, base, steps):
+    def share_first(cut, buffer, base, steps):
         for step in steps:
             push(share_across, cut, buffer, base, step)
+
+    def share_start(cut, buffer, base, steps):
+        share_first(cut, buffer, base, steps)
         push(share_near, cut, buffer, base)
 
     def share_on(cut, buffer, base, steps):
@@ -311,8 +327,9 @@
         share_near(cut, buffer, base).wait_recv()
 
     BOTH, ONE = (2, 3), (2,)
-
-    share_start(r.qkv_cut, r.qkv_own, ID_QKV, BOTH)
+    FIRST, SECOND = 2, 3
+
+    share_first(r.qkv_cut, r.qkv_own, ID_QKV, BOTH)
     gather_start(r.tokens, ID_TOKENS, 0)
     for row in range(8):
         r.vectors[shard, row : row + 1, :] = rounded(
@@ -341,6 +358,9 @@
     share_start(r.up_cut, r.up_own, ID_UP, BOTH)
     gather_start(r.tokens, ID_TOKENS, 1)
 
+    for step in (1, 2, 3):
+        cut_rows(step)
+    push(share_near, r.qkv_cut, r.qkv_own, ID_QKV)
     r.qkv_own[at(shard, SLICE), :] = r.qkv_cut[shard]
     share_on(r.qkv_cut, r.qkv_own, ID_QKV, BOTH)
     for load in cotangent_loads:
@@ -419,6 +439,7 @@
     share_on(r.up_cut, r.up_own, ID_UP, BOTH)
     attend(0, 1)
     mix_start(0)
+    gather_start(r.cotangent, ID_COTANGENT, FIRST)
     attend(1, 0)
     gather_near(r.tokens, ID_TOKENS, 1).wait_recv()
     project(1, 0)
@@ -427,7 +448,7 @@
     project(1, 1)
     attend(1, 1)
     mix_start(1)
-    gather_start(r.cotangent, ID_COTANGENT, 0)
+    gather_start(r.cotangent, ID_COTANGENT, SECOND)
     share_last(r.out_all, ID_OUT, ONE)
     share_last(r.up_own, ID_UP, BOTH)
     mix_forward(0)
@@ -511,13 +532,13 @@
 
     def feed(clip, kind, carry):
         rows = rows_of(kind)
-        if clip == 0:
-
-            @pl.when(kind == 1)
-            def _():
+
+        @pl.when(kind == 1)
+        def _():
+            for part in ((FIRST, SECOND), (1,))[clip]:
                 pass_on(
-                    gather_across(r.cotangent, ID_COTANGENT, 0),
-                    gather_on(r.cotangent, ID_COTANGENT, 0),
+                    gather_across(r.cotangent, ID_COTANGENT, part),
+                    gather_on(r.cotangent, ID_COTANGENT, part),
                 )
 
         total = to_single(r.tokens[clip, rows, :]) + whole(BO)
@@ -565,16 +586,17 @@
         lax.fori_loop(0, 2, functools.partial(step, clip), 0)
 
     both(feed, 0)
-    finals.append(functools.partial(gather_on, r.cotangent, ID_COTANGENT, 0))
-    gather_near(r.cotangent, ID_COTANGENT, 0).wait_recv()
-    gather_on(r.cotangent, ID_COTANGENT, 0).wait_recv()
+    for half in (FIRST, SECOND):
+        finals.append(functools.partial(gather_on, r.cotangent, ID_COTANGENT, half))
+        gather_near(r.cotangent, ID_COTANGENT, half).wait_recv()
+        gather_on(r.cotangent, ID_COTANGENT, half).wait_recv()
     both(feed_back, 0)
     finals.append(functools.partial(mix_on, 2))
     mix_near(2).wait_recv()
     mix_on(2).wait_recv()
     sum_on(0, ID_SUM_TWO, 0)
     both(feed, 1)
-    gather_forward(r.cotangent, ID_COTANGENT, 1)
+    finals.append(functools.partial(gather_on, r.cotangent, ID_COTANGENT, 1))
     gather_near(r.cotangent, ID_COTANGENT, 1).wait_recv()
     gather_on(r.cotangent, ID_COTANGENT, 1).wait_recv()
     stages = []
@@ -957,6 +979,17 @@
     r.small_all[0] = small_sum
     copies = grad_copies + [result_copy, local(r.small_all.at[0], r.small_out, 19)]
     copies[-1].start()
+    for item in finals:
+        item().wait_send()
+    for condition, item in conditional:
+        if condition is None:
+            item().wait_send()
+        else:
+
+            @pl.when(condition)
+            def _():
+                item().wait_send()
+
     run(106)
     copies.append(local(r.fulls[OUT], r.sums_out[OUT], 20))
     copies[-1].start()
@@ -969,17 +1002,6 @@
     run(56, 66, 76, 86, 96)
     copies.append(local(r.fulls[UP], r.sums_out[UP], 23))
     copies[-1].start()
-    for item in finals:
-        item().wait_send()
-    for condition, item in conditional:
-        if condition is None:
-            item().wait_send()
-        else:
-
-            @pl.when(condition)
-            def _():
-                item().wait_send()
-
     for item in copies:
         item.wait()
 

time: 137 us -> 135 us (0.985)
  Pallas kernels: 135 us -> 133 us
    pallas_call x1, Pallas kernels: 130 us -> 127 us  [layer(): pl.pallas_call(functools.partial(kernel, replicas, counted(inputs) + coun...]
where the time goes in v3:
time: 135 us; the launch traced here: 134 us
  Pallas kernels  133 us (99%)
  between operations  1.49 us (1%)
    pallas_call x1, Pallas kernels, layer(): pl.pallas_call(functools.partial(kernel, replicas, counted(inputs) + coun...  127 us
    pallas_call x1, Pallas kernels, layer(): pl.pallas_call(functools.partial(finish, counted(last_inputs) + counted(l...  5.86 us

profile of v3, /device:TPU:0, one launch (start us, length us, event | category | flops | bytes accessed | tf_op | source)
XLA Modules:
  0.0 134.5 jit_solution(12026188118723736475)
XLA Ops:
  1.3 127.1 %layer.1 = (bf16[2,128,768]{2,1,0:T(8,128)(2,1)}, f32[2,128,768]{2,1,0:T(8,128)}, f32[16,192]{1,0:T(8,128)}, bf16[4,192,768]{2,1,0:T(8,128)(2,1)}, bf16[4,192,76...) custom-call(bf16[2,128,768]{2,1,0:T(8,128)(2,1)} %refs_0_.1, ...), custom_call_target="tpu_custom_call" | custom-call | tf_op jit(solution)/shard_map/layer/pallas_call | solution.py:1188
  128.4 5.9 %finish.1 = (bf16[2,128,768]{2,1,0:T(8,128)(2,1)}, f32[2,128,768]{2,1,0:T(8,128)}, f32[768,768]{1,0:T(8,128)}, f32[192,3072]{1,0:T(8,128)}, f32[192,768]{1,0:T(8...) custom-call(bf16[2,128,768]{2,1,0:T(8,128)(2,1)} %get-tuple-element., ...), custom_call_target="tpu_custom_call" | custom-call | tf_op jit(solution)/shard_map/finish/pallas_call | solution.py:1219

commit v4 on v3

--- a/solution.py
+++ b/solution.py
@@ -817,7 +817,7 @@
         total = to_single(r.cotangent[clip, own, :]) + norm_back(
             grad_two, normal, scale, whole(G2)
         )
-        r.down_wide[4 * slot + clip * slot : 5 * slot + clip * slot, :] = total
+        r.input_grad_out[clip] = total
         r.gradient[clip, own, :] = total.astype(BRAIN)
         gather_start(r.gradient, ID_GRADIENT, clip)
         plan()
@@ -897,26 +897,14 @@
     for clip in (0, 1):
         live = 1.0 if clip == 0 else second_live
         result = r.middle_own[clip] + sum_end(1, ID_SUM_RESULT, clip) + whole(C2)
-        r.hidden_one[clip, 0:slot, :] = (result * live).astype(BRAIN)
-    result_copy = local(r.hidden_one.at[:, 0:slot, :], r.result_out, 17)
-    result_copy.start()
+        r.result_out[clip] = (result * live).astype(BRAIN)
     plan()
     for clip in (0, 1):
         grad_one = sum_end(0, ID_SUM_ONE, clip)
         normal, scale = normalize(to_single(r.tokens[clip, own, :]))
         r.columns[6:7, :] += row_sum(grad_one * normal)
         r.columns[7:8, :] += row_sum(grad_one)
-        r.down_wide[4 * slot + clip * slot : 5 * slot + clip * slot, :] += norm_back(grad_one, normal, scale, whole(G1))
-    grad_copies = [
-        local(
-            r.down_wide.at[4 * slot + clip * slot : 5 * slot + clip * slot],
-            r.input_grad_out.at[clip],
-            18 + 6 * clip,
-        )
-        for clip in (0, 1)
-    ]
-    for item in grad_copies:
-        item.start()
+        r.input_grad_out[clip] += norm_back(grad_one, normal, scale, whole(G1))
 
     for member in range(GROUP):
         cols = slice(member * SLICE, (member + 1) * SLICE)
@@ -976,9 +964,7 @@
     small_sum = r.small_all[0]
     for step in range(1, replicas):
         small_sum += r.small_all[step]
-    r.small_all[0] = small_sum
-    copies = grad_copies + [result_copy, local(r.small_all.at[0], r.small_out, 19)]
-    copies[-1].start()
+    r.small_out[...] = small_sum
     for item in finals:
         item().wait_send()
     for condition, item in conditional:
@@ -991,34 +977,17 @@
                 item().wait_send()
 
     run(106)
-    copies.append(local(r.fulls[OUT], r.sums_out[OUT], 20))
-    copies[-1].start()
     run(6, 16, 26, 36, 46)
-    copies.append(local(r.fulls[DOWN], r.sums_out[DOWN], 21))
-    copies[-1].start()
     run(116, 126, 136, 146, 156)
-    copies.append(local(r.fulls[QKVS], r.sums_out[QKVS], 22))
-    copies[-1].start()
     run(56, 66, 76, 86, 96)
-    copies.append(local(r.fulls[UP], r.sums_out[UP], 23))
-    copies[-1].start()
-    for item in copies:
-        item.wait()
 
 
 def finish(fields, *refs):
     r = gathered(fields, refs)
     units = []
 
-    def unit(source, held, wide, target, widen):
-        index = len(units)
-        units.append(
-            (
-                pltpu.make_async_copy(source, held, r.near.at[index]),
-                pltpu.make_async_copy(wide, target, r.near.at[index]),
-                widen,
-            )
-        )
+    def unit(wide, target, widen):
+        units.append((pltpu.make_async_copy(wide, target, r.near.at[len(units)]), widen))
 
     def keep():
         pass
@@ -1029,27 +998,18 @@
         def widen():
             r.wide[DOWN][rows, :] = to_single(r.narrow[DOWN][index])
 
-        unit(
-            r.sums_in[DOWN].at[index],
-            r.narrow[DOWN].at[index],
-            r.wide[DOWN].at[rows],
-            r.results[DOWN].at[rows],
-            widen,
-        )
+        unit(r.wide[DOWN].at[rows], r.results[DOWN].at[rows], widen)
 
     def up(index):
-        cols = slice(index * D, (index + 1) * D)
+        rows = slice(index * PIECE, (index + 1) * PIECE)
 
         def widen():
-            r.wide[UP][:, cols] = to_single(r.narrow[UP][index])
-
-        unit(
-            r.sums_in[UP].at[index],
-            r.narrow[UP].at[index],
-            r.wide[UP].at[:, cols],
-            r.results[UP].at[:, cols],
-            widen,
-        )
+            for member in range(GROUP):
+                r.wide[UP][rows, member * D : (member + 1) * D] = to_single(
+                    r.narrow[UP][member, rows, :]
+                )
+
+        unit(r.wide[UP].at[rows], r.results[UP].at[rows], widen)
 
     def qkv(index):
         rows = slice(index * PIECE, (index + 1) * PIECE)
@@ -1063,40 +1023,31 @@
                     )
                 )
 
-        unit(
-            r.sums_in[QKVS].at[:, rows],
-            r.narrow[QKVS].at[:, rows],
-            r.wide[QKVS].at[rows],
-            r.results[QKVS].at[rows],
-            widen,
-        )
+        unit(r.wide[QKVS].at[rows], r.results[QKVS].at[rows], widen)
 
     def out():
         def widen():
             r.wide[OUT][...] = to_single(r.narrow[OUT][0])
 
-        unit(r.sums_in[OUT], r.narrow[OUT], r.wide[OUT], r.results[OUT], widen)
-
-    unit(r.input_grad_in, r.input_grad_held, r.input_grad_held, r.input_grad, keep)
-    unit(r.result_in, r.result_held, r.result_held, r.result, keep)
+        unit(r.wide[OUT], r.results[OUT], widen)
+
+    unit(r.input_grad_in, r.input_grad, keep)
+    unit(r.result_in, r.result, keep)
     for index in range(GROUP):
         down(index)
         up(index)
     out()
     for index in range(GROUP):
         qkv(index)
-    for load, _, _ in units:
-        load.start()
     for row in range(8):
         r.vectors[row][...] = r.small_in[row : row + 1, :].reshape(SLICE)
     r.vectors[8][...] = jnp.concatenate(
         [r.small_in[C1 + part : C1 + part + 1, :] for part in range(GROUP)], 1
     ).reshape(D)
-    for load, store, widen in units:
-        load.wait()
+    for store, widen in units:
         widen()
         store.start()
-    for _, store, _ in units:
+    for store, _ in units:
         store.wait()
 
 
@@ -1113,7 +1064,6 @@
     )
     anywhere = pl.BlockSpec(memory_space=pl.ANY)
     in_memory = pl.BlockSpec(memory_space=pltpu.VMEM)
-    in_hbm = pl.BlockSpec(memory_space=pltpu.HBM)
     shape = jax.ShapeDtypeStruct
 
     inputs = dict(
@@ -1127,10 +1077,10 @@
         down_in=anywhere,
     )
     outputs = dict(
-        result_out=shape(tokens.shape, BRAIN),
-        input_grad_out=shape(tokens.shape, SINGLE),
-        small_out=shape((VECTOR_ROWS, SLICE), SINGLE),
-        sums_out=[shape((blocks, SLICE, columns), BRAIN) for blocks, columns, _, _ in WEIGHTS],
+        result_out=pltpu.VMEM(tokens.shape, BRAIN),
+        input_grad_out=pltpu.VMEM(tokens.shape, SINGLE),
+        small_out=pltpu.VMEM((VECTOR_ROWS, SLICE), SINGLE),
+        fulls=[pltpu.VMEM((blocks, SLICE, columns), BRAIN) for blocks, columns, _, _ in WEIGHTS],
     )
     scratch = dict(
         qkv_wide=pltpu.VMEM(qkv_weight.shape, SINGLE),
@@ -1173,7 +1123,6 @@
         halves=[pltpu.VMEM((w[0], PAIR, w[1]), BRAIN) for w in WEIGHTS],
         lines=[pltpu.VMEM((w[0], PAIR, w[1]), BRAIN) for w in WEIGHTS],
         middles=[pltpu.VMEM((w[0], PAIR, w[1]), BRAIN) for w in WEIGHTS],
-        fulls=[pltpu.VMEM((w[0], SLICE, w[1]), BRAIN) for w in WEIGHTS],
         crossed=[pltpu.VMEM((GROUP, PAIR, w[1]), BRAIN) for w in WEIGHTS if w[2]],
         extras=[
             pltpu.VMEM((levels, w[0], PAIR, w[1]) if levels else (1, 1, 16, TILE), BRAIN)
@@ -1189,10 +1138,10 @@
         functools.partial(kernel, replicas, counted(inputs) + counted(outputs) + counted(scratch)),
         out_shape=tuple(flat(outputs)),
         in_specs=flat(inputs),
-        out_specs=(anywhere,) * len(flat(outputs)),
+        out_specs=(in_memory,) * len(flat(outputs)),
         scratch_shapes=flat(scratch),
         compiler_params=pltpu.CompilerParams(
-            collective_id=0, has_side_effects=True, vmem_limit_bytes=65000 * 1024
+            collective_id=0, has_side_effects=True, vmem_limit_bytes=60600 * 1024
         ),
         name="layer",
     )(
@@ -1201,7 +1150,7 @@
 
     matrices = [fc2_weight, fc1_weight, out_weight, qkv_weight]
     last_inputs = dict(
-        result_in=in_hbm, input_grad_in=in_hbm, small_in=in_memory, sums_in=[in_hbm] * 4
+        result_in=in_memory, input_grad_in=in_memory, small_in=in_memory, narrow=[in_memory] * 4
     )
     last_outputs = dict(
         result=shape(tokens.shape, BRAIN),
@@ -1210,10 +1159,7 @@
         vectors=[shape(vector.shape, SINGLE) for vector in vectors],
     )
     last_scratch = dict(
-        narrow=[pltpu.VMEM((blocks, SLICE, columns), BRAIN) for blocks, columns, _, _ in WEIGHTS],
         wide=[pltpu.VMEM(array.shape, SINGLE) for array in matrices],
-        input_grad_held=pltpu.VMEM(tokens.shape, SINGLE),
-        result_held=pltpu.VMEM(tokens.shape, BRAIN),
         near=pltpu.SemaphoreType.DMA((16,)),
     )
     values = pl.pallas_call(
@@ -1224,7 +1170,7 @@
         in_specs=flat(last_inputs),
         out_specs=(anywhere,) * 6 + (in_memory,) * 9,
         scratch_shapes=flat(last_scratch),
-        compiler_params=pltpu.CompilerParams(vmem_limit_bytes=60 << 20),
+        compiler_params=pltpu.CompilerParams(vmem_limit_bytes=32 << 20),
         name="finish",
     )(*sums)
     o = gathered(counted(last_outputs), values)

time: 135 us -> 131 us (0.970)
  Pallas kernels: 133 us -> 129 us
    pallas_call x1, Pallas kernels: 5.86 us -> 4.01 us  [layer(): pl.pallas_call(functools.partial(finish, counted(last_inputs) + counted(l...]
    pallas_call x1, Pallas kernels: 127 us -> 125 us  [layer(): pl.pallas_call(functools.partial(kernel, replicas, counted(inputs) + coun...]
where the time goes in v4:
time: 131 us
  Pallas kernels  129 us (98%)
  between operations  1.49 us (1%)
    pallas_call x1, Pallas kernels, layer(): pl.pallas_call(functools.partial(kernel, replicas, counted(inputs) + coun...  125 us
    pallas_call x1, Pallas kernels, layer(): pl.pallas_call(functools.partial(finish, counted(last_inputs) + counted(l...  4.01 us

profile of v4, /device:TPU:0, one launch (start us, length us, event | category | flops | bytes accessed | tf_op | source)
XLA Modules:
  0.0 130.9 jit_solution(10516576854779339255)
XLA Ops:
  1.3 125.4 %layer.1 = (bf16[2,128,768]{2,1,0:T(8,128)(2,1)S(1)}, f32[2,128,768]{2,1,0:T(8,128)S(1)}, f32[16,192]{1,0:T(8,128)S(1)}, bf16[4,192,768]{2,1,0:T(8,128)(2,1)S(1)...) custom-call(bf16[2,128,768]{2,1,0:T(8,128)(2,1)} %refs_0_.1, ...), custom_call_target="tpu_custom_call" | custom-call | tf_op jit(solution)/shard_map/layer/pallas_call | solution.py:1137
  126.7 4.0 %finish.1 = (bf16[2,128,768]{2,1,0:T(8,128)(2,1)}, f32[2,128,768]{2,1,0:T(8,128)}, f32[768,768]{1,0:T(8,128)}, f32[192,3072]{1,0:T(8,128)}, f32[192,768]{1,0:T(8...) custom-call(bf16[2,128,768]{2,1,0:T(8,128)(2,1)S(1)} %get-tuple-elem, ...), custom_call_target="tpu_custom_call" | custom-call | tf_op jit(solution)/shard_map/finish/pallas_call | solution.py:1165

commit v5 on v4

--- a/solution.py
+++ b/solution.py
@@ -542,15 +542,29 @@
                 )
 
         total = to_single(r.tokens[clip, rows, :]) + whole(BO)
-        for member in range(GROUP):
+        for first in (0, 2):
             heads = jnp.concatenate(
+                [r.mixed[member, 2 * clip, rows, :] for member in (first, first + 1)], 1
+            )
+            weights = jnp.concatenate(
                 [
-                    r.mixed[member, 2 * clip, rows, :],
-                    r.mixed[member, 1, rows, clip * HD : (clip + 1) * HD],
+                    r.out_all[member * SLICE : member * SLICE + TILE, :]
+                    for member in (first, first + 1)
                 ],
-                1,
+                0,
             )
-            total += dot(heads, r.out_all[member * SLICE : (member + 1) * SLICE, :], 1, 0)
+            total += dot(heads, weights, 1, 0)
+        heads = jnp.concatenate(
+            [r.mixed[member, 1, rows, clip * HD : (clip + 1) * HD] for member in range(GROUP)], 1
+        )
+        weights = jnp.concatenate(
+            [
+                r.out_all[member * SLICE + TILE : (member + 1) * SLICE, :]
+                for member in range(GROUP)
+            ],
+            0,
+        )
+        total += dot(heads, weights, 1, 0)
 
         @pl.when(kind == 1)
         def _():

time: 131 us -> 131 us (level)
  no operation moved by 1% of the time
where the time goes in v5:
time: 131 us; the launch traced here: 130 us
  Pallas kernels  129 us (98%)
  between operations  1.49 us (1%)
    pallas_call x1, Pallas kernels, layer(): pl.pallas_call(functools.partial(kernel, replicas, counted(inputs) + coun...  125 us
    pallas_call x1, Pallas kernels, layer(): pl.pallas_call(functools.partial(finish, counted(last_inputs) + counted(l...  4.01 us

profile of v5, /device:TPU:0, one launch (start us, length us, event | category | flops | bytes accessed | tf_op | source)
XLA Modules:
  0.0 130.4 jit_solution(11840645056001720133)
XLA Ops:
  1.3 124.9 %layer.1 = (bf16[2,128,768]{2,1,0:T(8,128)(2,1)S(1)}, f32[2,128,768]{2,1,0:T(8,128)S(1)}, f32[16,192]{1,0:T(8,128)S(1)}, bf16[4,192,768]{2,1,0:T(8,128)(2,1)S(1)...) custom-call(bf16[2,128,768]{2,1,0:T(8,128)(2,1)} %refs_0_.1, ...), custom_call_target="tpu_custom_call" | custom-call | tf_op jit(solution)/shard_map/layer/pallas_call | solution.py:1151
  126.2 4.0 %finish.1 = (bf16[2,128,768]{2,1,0:T(8,128)(2,1)}, f32[2,128,768]{2,1,0:T(8,128)}, f32[768,768]{1,0:T(8,128)}, f32[192,3072]{1,0:T(8,128)}, f32[192,768]{1,0:T(8...) custom-call(bf16[2,128,768]{2,1,0:T(8,128)(2,1)S(1)} %get-tuple-elem, ...), custom_call_target="tpu_custom_call" | custom-call | tf_op jit(solution)/shard_map/finish/pallas_call | solution.py:1179

commit v6 on v5

--- a/solution.py
+++ b/solution.py
@@ -30,9 +30,11 @@
     (GROUP, D, False, ((0, 128, True), (128, 128, True), (256, 128, True), (384, 128, True), (512, 256, False))),
     (GROUP, D, True, ((0, 128, True), (128, 128, True), (256, 128, True), (384, 128, True), (512, 256, False))),
     (1, D, False, ((0, 768, False),)),
-    (GROUP, 640, True, ((0, 128, True), (128, 128, True), (256, 128, True), (384, 128, True), (512, 128, True))),
+    (GROUP, 512, True, ((0, 128, True), (128, 128, True), (256, 128, True), (384, 128, True))),
+    (2, 128, True, ((0, 128, True),)),
 )
-DOWN, UP, OUT, QKVS = range(4)
+DOWN, UP, OUT, QKVS, TAIL = range(5)
+TAIL_LEFT = 512
 ITEMS = sum(len(parts) for _, _, _, parts in WEIGHTS)
 
 MIXES = (((0, 0), (0, 1)), ((0, 2), (1, 2)), ((1, 0), (1, 1)))
@@ -622,6 +624,7 @@
         )
         crossed = r.crossed[index // 2] if crosses else None
         blocks = grad.shape[0]
+        share = full.shape[0] // blocks
         cols = slice(columns[0], columns[0] + columns[1])
         size = PAIR if y_first else PIECE
         first, first_peer, second, second_peer = (
@@ -672,7 +675,7 @@
 
         def cross_copy(step):
             return remote(
-                line.at[mate(step), 0:size, cols],
+                line.at[mate(step) // share, 0:size, cols],
                 crossed.at[shard, 0:size, cols],
                 base + 2 + step,
                 shard=mate(step),
@@ -728,7 +731,7 @@
                     + to_single(r.extras[index][level, :, 0:size, cols])
                 ).astype(BRAIN)
             if crosses:
-                crossed[shard, 0:size, cols] = line[shard, 0:size, cols]
+                crossed[shard, 0:size, cols] = line[shard // share, 0:size, cols]
                 for step in (2, 3, 1):
                     cross_copy(step).start()
 
@@ -738,7 +741,7 @@
                     cross_copy(step).wait()
             second_back().start()
             first_back(False).start()
-            for block in range(blocks):
+            for block in range(full.shape[0]):
                 full[block, final_rows(second), cols] = source[block]
             conditional.append((inner if y_first else None, second_back))
             conditional.append(
@@ -779,7 +782,7 @@
             )
         )
 
-    grads = (r.up_cut, r.up_grad, r.out_grad, r.qkv_grad)
+    grads = (r.up_cut, r.up_grad, r.out_grad, r.qkv_grad, r.tail_grad)
     for index, (_, _, crosses, parts) in enumerate(WEIGHTS):
         for start_column, width, y_first in parts:
             weight(index, len(stages), crosses, (start_column, width), y_first, grads[index])
@@ -804,10 +807,14 @@
                 0,
                 0,
             )
+            kept = min(width, target.shape[2])
             for half in range(2):
-                target[2 * part + half, :, 0:width] = product[
-                    half * SLICE : (half + 1) * SLICE
-                ].astype(BRAIN)
+                rows = slice(half * SLICE, (half + 1) * SLICE)
+                target[2 * part + half] = product[rows, 0:kept].astype(BRAIN)
+                if kept < width:
+                    r.tail_grad[part, :, half * HD : (half + 1) * HD] = product[
+                        rows, kept:width
+                    ].astype(BRAIN)
 
     steps = iter(PLAN)
 
@@ -892,7 +899,6 @@
     run(100)
     plan()
     cut_product(r.qkv_grad, r.hidden_one, r.pairs_grad, QKV)
-    r.qkv_grad[:, :, QKV:] = jnp.zeros((GROUP, SLICE, HD), BRAIN)
     run(110, 120, 130, 140, 150)
     plan()
 
@@ -998,6 +1004,7 @@
 
 def finish(fields, *refs):
     r = gathered(fields, refs)
+    odd = lax.axis_index("shard") % 2 == 1
     units = []
 
     def unit(wide, target, widen):
@@ -1030,12 +1037,14 @@
 
         def widen():
             for part in range(3):
-                cols = slice(part * SLICE, (part + 1) * SLICE)
-                r.wide[QKVS][rows, part * D : (part + 1) * D] = to_single(
-                    jnp.concatenate(
-                        [r.narrow[QKVS][member, rows, cols] for member in range(GROUP)], 1
-                    )
-                )
+                cols = slice(part * SLICE, min((part + 1) * SLICE, TAIL_LEFT))
+                pieces = []
+                for member in range(GROUP):
+                    pieces.append(to_single(r.narrow[QKVS][member, rows, cols]))
+                    if part == 2:
+                        last = to_single(r.narrow[TAIL][member, rows, :])
+                        pieces.append(jnp.where(odd, last[:, HD:], last[:, 0:HD]))
+                r.wide[QKVS][rows, part * D : (part + 1) * D] = jnp.concatenate(pieces, 1)
 
         unit(r.wide[QKVS].at[rows], r.results[QKVS].at[rows], widen)
 
@@ -1094,7 +1103,9 @@
         result_out=pltpu.VMEM(tokens.shape, BRAIN),
         input_grad_out=pltpu.VMEM(tokens.shape, SINGLE),
         small_out=pltpu.VMEM((VECTOR_ROWS, SLICE), SINGLE),
-        fulls=[pltpu.VMEM((blocks, SLICE, columns), BRAIN) for blocks, columns, _, _ in WEIGHTS],
+        fulls=[
+            pltpu.VMEM((GROUP if w[2] else w[0], SLICE, w[1]), BRAIN) for w in WEIGHTS
+        ],
     )
     scratch = dict(
         qkv_wide=pltpu.VMEM(qkv_weight.shape, SINGLE),
@@ -1129,7 +1140,8 @@
         sum_own=pltpu.VMEM((2, 2, slot, D), SINGLE),
         up_grad=pltpu.VMEM((GROUP, SLICE, D), BRAIN),
         out_grad=pltpu.VMEM((1, SLICE, D), BRAIN),
-        qkv_grad=pltpu.VMEM((GROUP, SLICE, QKV + HD), BRAIN),
+        qkv_grad=pltpu.VMEM((GROUP, SLICE, TAIL_LEFT), BRAIN),
+        tail_grad=pltpu.VMEM((2, SLICE, TILE), BRAIN),
         columns=pltpu.VMEM((8, D), SINGLE),
         small_sent=pltpu.VMEM((GROUP, 8, SLICE), SINGLE),
         small_near=pltpu.VMEM((GROUP - 1, 8, SLICE), SINGLE),
@@ -1164,7 +1176,7 @@
 
     matrices = [fc2_weight, fc1_weight, out_weight, qkv_weight]
     last_inputs = dict(
-        result_in=in_memory, input_grad_in=in_memory, small_in=in_memory, narrow=[in_memory] * 4
+        result_in=in_memory, input_grad_in=in_memory, small_in=in_memory, narrow=[in_memory] * len(WEIGHTS)
     )
     last_outputs = dict(
         result=shape(tokens.shape, BRAIN),

time: 131 us -> 131 us (level)
  no operation moved by 1% of the time
where the time goes in v6:
time: 131 us; the launch traced here: 130 us
  Pallas kernels  129 us (98%)
  between operations  1.49 us (1%)
    pallas_call x1, Pallas kernels, layer(): pl.pallas_call(functools.partial(kernel, replicas, counted(inputs) + coun...  125 us
    pallas_call x1, Pallas kernels, layer(): pl.pallas_call(functools.partial(finish, counted(last_inputs) + counted(l...  4.03 us

profile of v6, /device:TPU:0, one launch (start us, length us, event | category | flops | bytes accessed | tf_op | source)
XLA Modules:
  0.0 130.5 jit_solution(9383260559172464858)
XLA Ops:
  1.3 124.9 %layer.1 = (bf16[2,128,768]{2,1,0:T(8,128)(2,1)S(1)}, f32[2,128,768]{2,1,0:T(8,128)S(1)}, f32[16,192]{1,0:T(8,128)S(1)}, bf16[4,192,768]{2,1,0:T(8,128)(2,1)S(1)...) custom-call(bf16[2,128,768]{2,1,0:T(8,128)(2,1)} %refs_0_.1, ...), custom_call_target="tpu_custom_call" | custom-call | tf_op jit(solution)/shard_map/layer/pallas_call | solution.py:1163
  126.2 4.0 %finish.1 = (bf16[2,128,768]{2,1,0:T(8,128)(2,1)}, f32[2,128,768]{2,1,0:T(8,128)}, f32[768,768]{1,0:T(8,128)}, f32[192,3072]{1,0:T(8,128)}, f32[192,768]{1,0:T(8...) custom-call(bf16[2,128,768]{2,1,0:T(8,128)(2,1)S(1)} %get-tuple-elem, ...), custom_call_target="tpu_custom_call" | custom-call | tf_op jit(solution)/shard_map/finish/pallas_call | solution.py:1191
